TPU v7x, 128 devices: a whole 4x4x4 slice. The times are simulated.
128 devices in a mesh: section: 4 (over y), expert: 32 (over x, z, core).
Axes of the slice: x: 4, y: 4, z: 4, core: 2. Of those that a mesh axis runs over, the one named last changes fastest.
Arguments:
- upstream_dy: bfloat16 [4, 2, 2048, 6144], P('section', None, 'expert'), may hold values from -6 to 6
- gate_logits: float32 [4, 2, 2048, 2], P('section', None, 'expert'), may hold values from -8 to 8
- expert_ids: int32 [4, 2, 2048, 2], P('section', None, 'expert'), may hold values from 0 to 3, all different within a row; in each aligned block of 64 rows (0 to 63, 64 to 127, ..., all dimensions but the last counted through in order) at most 36 rows name the same one
- saved_hidden: bfloat16 [4, 2, 32, 36, 32768], P('section', None, None, None, 'expert'), may hold values from -6 to 6
- down_weight: bfloat16 [4, 32768, 6144], P('section', 'expert'), may hold values from -0.0625 to 0.0625
- router_weight: float32 [4, 6144, 4], P('section'), may hold values from -0.078125 to 0.078125
Outputs:
- hidden_grad: bfloat16 [4, 2, 32, 36, 32768], P('section', None, None, None, 'expert')
- upstream_grad: bfloat16 [4, 2, 2048, 6144], P('section', None, 'expert')
Inputs may be any that keep to these rules, and one draw needn't show every extreme that they name: `expert_ids`: the two experts of a token differ. In each device's block of 64 tokens of one microbatch no expert is named by more than 36 tokens, a bound that some block reaches.
All inputs are finite; a program needn't handle non-finite values.
Results may differ from a plain program's by a relative error of at most 0.0045.
Values may be sent and summed in bfloat16 or wider, within the bound.
A program may use at most 192 MiB of HBM per device.

v0:
```python
import jax
import jax.numpy as jnp
from jax import lax
from jax.sharding import PartitionSpec as P

EXPERTS = 4
CAP = 36


def passed_along(value, axis, steps):
    count = lax.axis_size(axis)
    leading, last = (max(0, -steps), min(count, count - steps))
    return lax.ppermute(value, axis, [(source, source + steps) for source in range(leading, last)])


def route_plan(out_grad, logits, chosen):
    highest = lax.Precision.HIGHEST
    gate_prob = jax.nn.sigmoid(logits - logits[:, ::-1])
    onehot = (chosen[:, :, None] == jnp.arange(EXPERTS, dtype=jnp.int32)).astype(jnp.float32)
    picked = jnp.sum(onehot, axis=1)
    slot_rank = jnp.cumsum(picked, axis=0) - picked
    slot_index = jnp.arange(CAP).astype(jnp.float32)
    select = picked[None] * (slot_rank[None] == slot_index[:, None, None]).astype(jnp.float32)
    copies = jnp.einsum(
        "cte,td->ecd", select.astype(jnp.bfloat16), out_grad, preferred_element_type=jnp.float32
    ).astype(jnp.bfloat16)
    gate_expert = jnp.sum(onehot * gate_prob[:, :, None], axis=1)
    slot_gate = jnp.einsum("cte,te->ec", select, gate_expert, precision=highest).astype(
        jnp.bfloat16
    )
    return (copies, slot_gate, select, onehot, gate_prob)


def expert_part(got_rows, got_gates, saved, weight):
    flat_rows = got_rows.reshape(-1, got_rows.shape[-1])
    hidden_raw = jnp.einsum(
        "rd,hd->rh", flat_rows, weight, preferred_element_type=jnp.float32
    ).reshape(saved.shape)
    grad = (got_gates.astype(jnp.float32)[:, :, None] * hidden_raw).astype(jnp.bfloat16)
    partial_value = jnp.sum(hidden_raw * saved.astype(jnp.float32), axis=-1)
    return (grad, partial_value)


def finish(partial_value, routing, out_grad, router_mat, groups):
    highest = lax.Precision.HIGHEST
    returned = lax.all_to_all(partial_value, "expert", split_axis=0, concat_axis=0, tiled=True)
    per_expert = jnp.sum(returned.reshape(EXPERTS, groups, returned.shape[-1]), axis=1)
    select = routing[2]
    onehot = routing[3]
    gate_prob = routing[4]
    token_part = jnp.einsum("cte,ec->te", select, per_expert, precision=highest)
    pair_part = jnp.sum(onehot * token_part[:, None, :], axis=-1)
    mixed = jnp.sum(gate_prob * pair_part, axis=-1, keepdims=True)
    logit_grad = gate_prob * (pair_part - mixed)
    spread = jnp.sum(onehot * logit_grad[:, :, None], axis=1)
    router_term = jnp.einsum("te,de->td", spread, router_mat, precision=highest)
    return (out_grad.astype(jnp.float32) + router_term).astype(jnp.bfloat16)


def local(upstream_dy, gate_logits, expert_ids, saved_hidden, down_weight, router_weight):
    groups = lax.axis_size("expert") // EXPERTS
    weight = down_weight[0]
    router_mat = router_weight[0]
    micro_count = upstream_dy.shape[1]
    routing_all = [
        route_plan(upstream_dy[0, micro_id], gate_logits[0, micro_id], expert_ids[0, micro_id])
        for micro_id in range(micro_count)
    ]
    arrived = [
        (
            lax.all_to_all(
                jnp.repeat(routing[0], groups, axis=0),
                "expert",
                split_axis=0,
                concat_axis=0,
                tiled=True,
            ),
            lax.all_to_all(
                jnp.repeat(routing[1], groups, axis=0),
                "expert",
                split_axis=0,
                concat_axis=0,
                tiled=True,
            ),
        )
        for routing in routing_all
    ]
    hidden_grads = []
    handoffs = []
    for micro_id in range(micro_count):
        grad, partial_value = expert_part(
            arrived[micro_id][0], arrived[micro_id][1], saved_hidden[0, micro_id], weight
        )
        hidden_grads.append(grad)
        input_grad = finish(
            partial_value, routing_all[micro_id], upstream_dy[0, micro_id], router_mat, groups
        )
        handoffs.append(input_grad)
    stacked = jnp.stack(handoffs)
    upstream = passed_along(stacked, "section", -1)
    return (jnp.stack(hidden_grads)[None], upstream[None])


def solution(mesh):
    placed = (
        P("section", None, "expert", None),
        P("section", None, "expert", None),
        P("section", None, "expert", None),
        P("section", None, None, None, "expert"),
        P("section", "expert", None),
        P("section", None, None),
    )
    return jax.shard_map(
        local,
        mesh=mesh,
        in_specs=placed,
        out_specs=(P("section", None, None, None, "expert"), P("section", None, "expert", None)),
        check_vma=False,
    )
```

profile of v0, /device:TPU:1, one launch (start us, length us, event | category | flops | bytes accessed | tf_op | source)
XLA Modules:
  0.0 623.2 jit_solution(12466059049630050526)
XLA Ops:
  0.7 0.7 slice_bitcast_fusion.3
  1.7 1.9 fusion.4
  3.5 5.8 broadcast_in_dim.13
  9.4 9.5 %all-to-all-start.1 = ((bf16[32,36,6144]{2,1,0:T(8,128)(2,1)}), bf16[32,36,6144]{2,1,0:T(8,128)(2,1)}, u32[]{:S(2)}, u32[]{:S(2)}) async-start(bf16[32,36,6144]{2,1,0:T(8,128)(2,1)} %bitcast.115), calls=%async_computation.1 | async-start | bytes 31457280 | tf_op jit(solution)/shard_map/all_to_all | solution.py:71
  19.2 1.9 fusion.5
  21.0 215.1 %all-to-all-done.1 = bf16[32,36,6144]{2,1,0:T(8,128)(2,1)} async-done(((bf16[32,36,6144]{2,1,0:T(8,128)(2,1)}), bf16[32,36,6144]{2,1,0:T(8,128)(2,1)}, u32[]{:S(2)}, u32[]{:S(2)}) %all-to-all-start.1) | async-done | bytes 14155808 | tf_op jit(solution)/shard_map/all_to_all | solution.py:71
  236.1 5.7 broadcast_in_dim.15
  241.8 40.0 %all-to-all-start.3 = ((bf16[32,36,6144]{2,1,0:T(8,128)(2,1)}), bf16[32,36,6144]{2,1,0:T(8,128)(2,1)}, u32[]{:S(2)}, u32[]{:S(2)}) async-start(bf16[32,36,6144]{2,1,0:T(8,128)(2,1)} %bitcast.114), calls=%async_computation.3 | async-start | bytes 31457280 | tf_op jit(solution)/shard_map/all_to_all | solution.py:71
  281.9 4.5 fusion.62
  286.3 27.0 %fusion.11 = (f32[32,36]{1,0:T(8,128)}, f32[32,36,1024]{2,1,0:T(8,128)}) fusion(bf16[1,1,32,36,1024]{4,2,3,1,0:T(8,128)(2,1)S(1)} %get-tuple-element.18, bf16[32,36,6144]{2,1,0:T(8,128)(2,1)} %all-to-all-done.1, bf16[1,1024,6144]{2,1,0:T(8,128)(2,1)} %param.10), kind=kOutput, calls=%fused_computation.18 | convolution fusion | flops 14499052544 | bytes 33821184 | tf_op jit(solution)/shard_map/rd,hd->rh/dot_general | solution.py:36
  313.3 185.7 %all-to-all-done.3 = bf16[32,36,6144]{2,1,0:T(8,128)(2,1)} async-done(((bf16[32,36,6144]{2,1,0:T(8,128)(2,1)}), bf16[32,36,6144]{2,1,0:T(8,128)(2,1)}, u32[]{:S(2)}, u32[]{:S(2)}) %all-to-all-start.3) | async-done | bytes 14155808 | tf_op jit(solution)/shard_map/all_to_all | solution.py:71
  499.0 39.9 %all-to-all-start.4 = ((f32[32,1,36]{2,1,0:T(1,128)}), f32[32,1,36]{2,1,0:T(1,128)S(1)}, u32[]{:S(2)}, u32[]{:S(2)}) async-start(f32[32,1,36]{2,1,0:T(1,128)} %bitcast.30), calls=%async_computation.4 | async-start | bytes 32768 | tf_op jit(solution)/shard_map/all_to_all | solution.py:46
  538.9 26.4 %fusion.10 = (f32[32,36]{1,0:T(8,128)}, f32[32,36,1024]{2,1,0:T(8,128)}) fusion(bf16[1,1,32,36,1024]{4,2,3,1,0:T(8,128)(2,1)} %get-tuple-element.19, bf16[32,36,6144]{2,1,0:T(8,128)(2,1)} %all-to-all-done.3, bf16[1,1024,6144]{2,1,0:T(8,128)(2,1)} %param.10), kind=kOutput, calls=%fused_computation.16 | convolution fusion | flops 14499052544 | bytes 33821184 | tf_op jit(solution)/shard_map/rd,hd->rh/dot_general | solution.py:36
  565.3 7.4 %all-to-all-start.5 = ((f32[32,1,36]{2,1,0:T(1,128)}), f32[32,1,36]{2,1,0:T(1,128)S(1)}, u32[]{:S(2)}, u32[]{:S(2)}) async-start(f32[32,1,36]{2,1,0:T(1,128)} %bitcast.40), calls=%async_computation.5 | async-start | bytes 32768 | tf_op jit(solution)/shard_map/all_to_all | solution.py:46
  573.0 6.6 %all-to-all-done.5 = f32[32,1,36]{2,1,0:T(1,128)S(1)} async-done(((f32[32,1,36]{2,1,0:T(1,128)}), f32[32,1,36]{2,1,0:T(1,128)S(1)}, u32[]{:S(2)}, u32[]{:S(2)}) %all-to-all-start.5) | async-done | bytes 4640 | tf_op jit(solution)/shard_map/all_to_all | solution.py:46
  580.0 1.5 fusion.8
  581.5 1.5 fusion.9
  583.1 1.4 collective-permute-start
  584.6 0.3 fusion.24
  584.9 0.6 copy.52
  585.5 4.1 all-to-all-start
  590.0 0.6 copy.56
  590.6 6.0 all-to-all-done
  596.7 4.1 all-to-all-start.2
  600.9 7.0 %all-to-all-done.2 = bf16[32,1,36]{2,1,0:T(2,128)(2,1)S(1)} async-done(((bf16[32,1,36]{2,1,0:T(2,128)(2,1)}), bf16[32,1,36]{2,1,0:T(2,128)(2,1)S(1)}, u32[]{:S(2)}, u32[]{:S(2)}) %all-to-all-start.2) | async-done | bytes 2336 | tf_op jit(solution)/shard_map/all_to_all | solution.py:78
  607.9 3.0 fusion.12
  610.9 0.7 slice-done.1
  611.6 0.3 fusion.13
  611.9 0.5 maximum_bitcast_fusion
  612.5 4.8 copy.59
  617.3 3.3 collective-permute-done
  620.6 2.7 copy.77
  (43 shorter events, 1.8 us)
Async XLA Ops:
  0.6 579.4 %copy-start = (f32[1,6144,4]{1,2,0:T(4,128)S(1)}, f32[1,6144,4]{1,2,0:T(4,128)}, u32[]{:S(2)}) copy-start(f32[1,6144,4]{1,2,0:T(4,128)} %param.11) | copy-start | bytes 294916
  9.4 226.7 %all-to-all-start.1 = ((bf16[32,36,6144]{2,1,0:T(8,128)(2,1)}), bf16[32,36,6144]{2,1,0:T(8,128)(2,1)}, u32[]{:S(2)}, u32[]{:S(2)}) async-start(bf16[32,36,6144]{2,1,0:T(8,128)(2,1)} %bitcast.115), calls=%async_computation.1 | async-start | bytes 31457280 | tf_op jit(solution)/shard_map/all_to_all | solution.py:71
  241.8 40.0 %copy-start.2 = (f32[1,2,64,2]{2,3,1,0:T(2,128)S(1)}, f32[1,2,64,2]{2,3,1,0:T(2,128)}, u32[]{:S(2)}) copy-start(f32[1,2,64,2]{2,3,1,0:T(2,128)} %param.7) | copy-start | bytes 3076
  241.8 257.2 %all-to-all-start.3 = ((bf16[32,36,6144]{2,1,0:T(8,128)(2,1)}), bf16[32,36,6144]{2,1,0:T(8,128)(2,1)}, u32[]{:S(2)}, u32[]{:S(2)}) async-start(bf16[32,36,6144]{2,1,0:T(8,128)(2,1)} %bitcast.114), calls=%async_computation.3 | async-start | bytes 31457280 | tf_op jit(solution)/shard_map/all_to_all | solution.py:71
  499.0 66.3 %all-to-all-start.4 = ((f32[32,1,36]{2,1,0:T(1,128)}), f32[32,1,36]{2,1,0:T(1,128)S(1)}, u32[]{:S(2)}, u32[]{:S(2)}) async-start(f32[32,1,36]{2,1,0:T(1,128)} %bitcast.30), calls=%async_computation.4 | async-start | bytes 32768 | tf_op jit(solution)/shard_map/all_to_all | solution.py:46
  538.9 41.1 %copy-start.1 = (bf16[1,2,64,6144]{3,2,1,0:T(8,128)(2,1)S(1)}, bf16[1,2,64,6144]{3,2,1,0:T(8,128)(2,1)}, u32[]{:S(2)}) copy-start(bf16[1,2,64,6144]{3,2,1,0:T(8,128)(2,1)} %param.6) | copy-start | bytes 4718596
  565.3 14.3 %all-to-all-start.5 = ((f32[32,1,36]{2,1,0:T(1,128)}), f32[32,1,36]{2,1,0:T(1,128)S(1)}, u32[]{:S(2)}, u32[]{:S(2)}) async-start(f32[32,1,36]{2,1,0:T(1,128)} %bitcast.40), calls=%async_computation.5 | async-start | bytes 32768 | tf_op jit(solution)/shard_map/all_to_all | solution.py:46
  583.0 27.9 %slice-start = ((s8[5242880]{0:T(1024)(128)(4,1)}), s8[1048576]{0:T(1024)(128)(4,1)S(1)}, s32[]{:S(2)}) async-start(s8[5242880]{0:T(1024)(128)(4,1)} %bitcast.116), calls=%async_computation.6 | async-start | bytes 2097152
  583.1 37.4 %collective-permute-start = (bf16[2,64,6144]{2,1,0:T(8,128)(2,1)S(1)}, bf16[2,64,6144]{2,1,0:T(8,128)(2,1)}, u32[]{:S(2)}, u32[]{:S(2)}) collective-permute-start(bf16[2,64,6144]{2,1,0:T(8,128)(2,1)S(1)} %pad_maximum_fusion), channel_id=1, source_target_pairs={{32,0},{64,32},{96,64},{33,1},{65,33},{97,65},{34,2},{66,34},{98,6... | collective-permute-start | bytes 4718600 | tf_op jit(solution)/shard_map/ppermute | solution.py:13
  585.5 11.2 %all-to-all-start = ((bf16[32,1,36]{2,1,0:T(2,128)(2,1)}), bf16[32,1,36]{2,1,0:T(2,128)(2,1)S(1)}, u32[]{:S(2)}, u32[]{:S(2)}) async-start(bf16[32,1,36]{2,1,0:T(2,128)(2,1)} %copy.52), calls=%async_computation | async-start | bytes 32768 | tf_op jit(solution)/shard_map/all_to_all | solution.py:78
  596.7 11.2 %all-to-all-start.2 = ((bf16[32,1,36]{2,1,0:T(2,128)(2,1)}), bf16[32,1,36]{2,1,0:T(2,128)(2,1)S(1)}, u32[]{:S(2)}, u32[]{:S(2)}) async-start(bf16[32,1,36]{2,1,0:T(2,128)(2,1)} %copy.56), calls=%async_computation.2 | async-start | bytes 32768 | tf_op jit(solution)/shard_map/all_to_all | solution.py:78
  607.9 3.7 slice-start.1
where the time goes:
time: 624 us; the launch traced here: 623 us
  waiting for transfers between devices  424 us (68%)
  starting transfers between devices  106 us (17%)
  matrix products  61.2 us (10%)
  local copies, waits for them, and re-layouts  26.7 us (4%)
    all_to_all x2, waiting for transfers between devices, local(): lax.all_to_all(jnp.repeat(routing[0], groups, axis=0), 'expert', split_ax...  401 us
    dot_general x2, matrix products, expert_part(): jnp.einsum('rd,hd->rh', flat_rows, weight, preferred_element_type=jnp.flo...  53.4 us
    all_to_all x2, starting transfers between devices, local(): lax.all_to_all(jnp.repeat(routing[0], groups, axis=0), 'expert', split_ax...  49.5 us
    all_to_all x2, starting transfers between devices, finish(): lax.all_to_all(partial_value, 'expert', split_axis=0, concat_axis=0, tile...  47.2 us
    all_to_all x2, waiting for transfers between devices, local(): lax.all_to_all(jnp.repeat(routing[1], groups, axis=0), 'expert', split_ax...  13 us
  transfers between devices with their start and end apart: 7, of which 6 were waited for; matrix products, arithmetic and copies ran while one was open for 11% of the time, Pallas kernels for 0%

commit v1 on v0

v1 whole, which is shorter than its diff:
```python
import functools

import jax
import jax.numpy as jnp
from jax import lax
from jax.experimental import pallas as pl
from jax.experimental.pallas import tpu as pltpu
from jax.sharding import PartitionSpec as P

EXPERTS = 4
CAP = 36
NX = 4
NZ = 4
NC = 6
SRC = 2
ROWS = 16
MESH = pl.DeviceIdType.MESH
F32 = jnp.float32
BF16 = jnp.bfloat16


def permutation():
    i = lax.broadcasted_iota(jnp.int32, (256, 256), 0)
    n = lax.broadcasted_iota(jnp.int32, (256, 256), 1)
    z, x, src, slot = i >> 6, (i >> 4) & 3, (i >> 3) & 1, i & 7
    return (n == slot * 32 + (x * 4 + z) * 2 + src).astype(F32).astype(BF16)


def expert_kernel(
    groups, width, x_hbm, ct_hbm, saved_hbm, w_hbm, grad_hbm, part_ref,
    rows, wv, acc, sv, x2, ct2, sel, packed, gs, gt,
    x_sem, w_sem, s_sem, o_sem, loc_sem, b0_send, b0_recv, xs, xr, zs, zr, bs, br,
):
    me = lax.axis_index("expert")
    mx, mz, mc = me // 8, (me // 2) % 4, me % 2
    half = width * NC

    def dev(x, z, c):
        return {"expert": (lax.rem(x + 8, NX) * NZ + lax.rem(z + 8, NZ)) * 2 + c}

    sibling = dev(mx, mz, 1 - mc)
    xdev = [dev(mx + d, mz, mc) for d in range(NX)]
    zup, zdown = dev(mx, mz + 1, mc), dev(mx, mz - 1, mc)

    barrier = pltpu.get_barrier_semaphore()
    for target in (sibling, xdev[1], xdev[2], xdev[3], zup, zdown):
        pl.semaphore_signal(barrier, inc=1, device_id=target, device_id_type=MESH)
    pl.semaphore_wait(barrier, 6)

    def remote(src, dst, send, recv, target):
        return pltpu.make_async_remote_copy(
            src_ref=src, dst_ref=dst, send_sem=send, recv_sem=recv, device_id=target, device_id_type=MESH
        )

    mine = pl.ds(pl.multiple_of(mc * half, 128), half)
    other = pl.ds(pl.multiple_of((1 - mc) * half, 128), half)
    mine_rows = pl.ds(pl.multiple_of(mc * 128, 128), 128)
    sib_rows = pl.ds(pl.multiple_of((1 - mc) * 128, 128), 128)
    swap_x = remote(x_hbm.at[:, other], x2.at[mine_rows, :], b0_send.at[0], b0_recv.at[0], sibling)
    swap_c = remote(ct_hbm, ct2.at[mc], b0_send.at[1], b0_recv.at[1], sibling)
    own_x = pltpu.make_async_copy(x_hbm.at[:, mine], x2.at[mine_rows, :], x_sem.at[0])
    own_c = pltpu.make_async_copy(ct_hbm, ct2.at[mc], x_sem.at[1])
    for copy in (swap_c, swap_x, own_c, own_x):
        copy.start()
    w_copy = {}
    for k in range(NC):
        for h in range(2):
            cols = pl.ds(h * half + k * width, width)
            w_copy[k, h] = pltpu.make_async_copy(w_hbm.at[:, cols], wv.at[:, cols], w_sem.at[k, h])
            w_copy[k, h].start()
    s_copy = [pltpu.make_async_copy(saved_hbm.at[g], sv.at[g], s_sem.at[g]) for g in range(groups)]
    for copy in s_copy:
        copy.start()

    gs[...] = jnp.zeros_like(gs)
    own_c.wait()
    swap_c.wait_recv()
    for e in range(EXPERTS):
        code = jnp.concatenate([ct2[0, e : e + 1, :], ct2[1, e : e + 1, :]], axis=1)
        gate = jnp.concatenate([ct2[0, 4 + e : 5 + e, :], ct2[1, 4 + e : 5 + e, :]], axis=1)
        row = lax.broadcasted_iota(jnp.int32, (groups * ROWS, 256), 0).astype(F32)
        chosen = (row == code).astype(F32).astype(BF16)
        sel[e] = chosen
        gs[e, :, 0 : groups * ROWS] = lax.dot_general(
            jnp.broadcast_to(gate, (8, 256)).astype(BF16), chosen, (((1,), (1,)), ((), ())),
            preferred_element_type=F32,
        )
    own_x.wait()
    swap_x.wait_recv()

    chip = mz * NX + mx

    def group(k, h, z):
        return rows.at[k, h, :, pl.ds(lax.rem(z + 8, NZ) * NX, NX)]

    def gate_group(z):
        return gt.at[pl.ds(lax.rem(z + 8, NZ) * NX, NX)]

    def pack(k):
        for e in range(EXPERTS):
            block = jnp.dot(sel[e], x2[:, k * width : (k + 1) * width], preferred_element_type=F32)
            packed[k, e] = block.astype(BF16).reshape(groups, ROWS, width)

    waits = []

    def start_x(k):
        local = pltpu.make_async_copy(packed.at[k, mx], rows.at[k, mc, :, chip], loc_sem.at[k])
        local.start()
        for d in (2, 1, 3):
            e = lax.rem(mx + d, NX)
            copy = remote(packed.at[k, e], rows.at[k, mc, :, chip], xs.at[k, d - 1], xr.at[k, d - 1], xdev[d])
            copy.start()
            waits.append(copy)
        return local

    def arrived(ref, sem):
        remote(ref, ref, bs.at[0, 0], sem, sibling).wait_recv()

    def to_sibling(k, which, z):
        copy = remote(group(k, mc, z), group(k, mc, z), bs.at[k, which], br.at[k, which], sibling)
        copy.start()
        waits.append(copy)

    def z_send(ref, k, which, target):
        copy = remote(ref, ref, zs.at[k, which], zr.at[k, which], target)
        copy.start()
        waits.append(copy)

    def gates_x():
        local = pltpu.make_async_copy(gs.at[mx], gt.at[chip], loc_sem.at[NC])
        local.start()
        for d in (1, 2, 3):
            e = lax.rem(mx + d, NX)
            copy = remote(gs.at[e], gt.at[chip], xs.at[NC, d - 1], xr.at[NC, d - 1], xdev[d])
            copy.start()
            waits.append(copy)
        return local

    def stage_b(k, local):
        local.wait()
        for d in (1, 2, 3):
            source = mz * NX + lax.rem(mx - d + NX, NX)
            ref = rows.at[k, mc, :, source] if k < NC else gt.at[source]
            arrived(ref, xr.at[k, d - 1])
        ref = group(k, mc, mz) if k < NC else gate_group(mz)
        z_send(ref, k, 0, zup)
        z_send(ref, k, 1, zdown)
        if k < NC:
            to_sibling(k, 0, mz)

    def stage_c(k):
        below = group(k, mc, mz - 1) if k < NC else gate_group(mz - 1)
        above = group(k, mc, mz + 1) if k < NC else gate_group(mz + 1)

        def take_below():
            arrived(below, zr.at[k, 0])
            if k % 2 == 0:
                z_send(below, k, 2, zup)
            if k < NC:
                to_sibling(k, 1, mz - 1)

        def take_above():
            arrived(above, zr.at[k, 1])
            if k % 2 == 1:
                z_send(above, k, 2, zdown)
            if k < NC:
                to_sibling(k, 2, mz + 1)

        take_below()
        take_above()

    def stage_d(k):
        arrived(group(k, mc, mz + 2) if k < NC else gate_group(mz + 2), zr.at[k, 2])
        if k < NC:
            to_sibling(k, 3, mz + 2)

    big = groups // 3

    def compute(k):
        for which, z in enumerate((mz, mz - 1, mz + 1, mz + 2)):
            arrived(group(k, 1 - mc, z), br.at[k, which])
        for h in range(2):
            w_copy[k, h].wait()

        def body(m, carry):
            at = pl.ds(m * big, big)
            total = None
            for h in range(2):
                left = rows[k, h, at].reshape(big * 256, width)
                right = wv[:, h * half + k * width : h * half + (k + 1) * width]
                term = lax.dot_general(left, right, (((1,), (1,)), ((), ())), preferred_element_type=F32)
                total = term if total is None else total + term
            total = total.reshape(big, 256, total.shape[-1])
            acc[at] = total if k == 0 else acc[at] + total
            return carry

        lax.fori_loop(0, 3, body, 0)

    pack(0)
    pack(1)
    locals_ = {0: start_x(0)}
    locals_[NC] = gates_x()
    locals_[1] = start_x(1)
    for k in range(2, NC):
        pack(k)
        locals_[k] = start_x(k)
    perm = permutation()

    def place_saved(g, carry):
        sv[g] = jnp.dot(perm, sv[g], preferred_element_type=F32).astype(BF16)
        return carry

    for step in range(NC + 3):
        if step < NC:
            stage_b(step, locals_[step])
        if step == 1:
            stage_b(NC, locals_[NC])
        if 0 <= step - 1 < NC:
            stage_c(step - 1)
        if step == 2:
            stage_c(NC)
        if 0 <= step - 2 < NC:
            stage_d(step - 2)
        if step == 3:
            stage_d(NC)
        if step == 0:
            for copy in s_copy:
                copy.wait()
            lax.fori_loop(0, groups, place_saved, 0)
        if 0 <= step - 3 < NC:
            compute(step - 3)

    lane = lax.broadcasted_iota(jnp.int32, (256, 256), 1)
    row16 = lax.broadcasted_iota(jnp.int32, (256, 256), 0) & 15
    gates = jnp.broadcast_to(gt[:, 0:1, :], (16, 16, 256)).reshape(256, 256)
    part_ref[...] = jnp.zeros_like(part_ref)

    def finish(g, carry):
        place = lane == row16 + g * 16
        gate = jnp.sum(jnp.where(place, gates, 0.0), axis=1, keepdims=True)
        raw = acc[g]
        dots = jnp.sum(raw * sv[g].astype(F32), axis=1, keepdims=True)
        sv[g] = (gate * raw).astype(BF16)
        pltpu.make_async_copy(sv.at[g], grad_hbm.at[g], o_sem.at[g]).start()
        spread = jnp.where(place, dots, 0.0).reshape(16, 16, 256)
        part_ref[...] += jnp.sum(spread, axis=1)
        return carry

    lax.fori_loop(0, groups, finish, 0)
    for g in range(groups):
        pltpu.make_async_copy(sv.at[g], grad_hbm.at[g], o_sem.at[g]).wait()
    swap_c.wait_send()
    swap_x.wait_send()
    for copy in waits:
        copy.wait_send()


def expert_call(tokens, codes, saved, weight):
    depth, hidden = tokens.shape[-1], weight.shape[0]
    groups = saved.shape[0]
    width = depth // 2 // NC
    dma = pltpu.SemaphoreType.DMA
    return pl.pallas_call(
        functools.partial(expert_kernel, groups, width),
        name="experts",
        out_shape=(
            jax.ShapeDtypeStruct((groups, 256, hidden), BF16),
            jax.ShapeDtypeStruct((16, 256), F32),
        ),
        in_specs=[pl.BlockSpec(memory_space=pl.ANY)] * 4,
        out_specs=(pl.BlockSpec(memory_space=pl.ANY), pl.BlockSpec(memory_space=pltpu.VMEM)),
        scratch_shapes=[
            pltpu.VMEM((NC, 2, groups, 16, ROWS, width), BF16),
            pltpu.VMEM((hidden, depth), BF16),
            pltpu.VMEM((groups, 256, hidden), F32),
            pltpu.VMEM((groups, 256, hidden), BF16),
            pltpu.VMEM((256, depth // 2), BF16),
            pltpu.VMEM((2, 8, 128), F32),
            pltpu.VMEM((EXPERTS, groups * ROWS, 256), BF16),
            pltpu.VMEM((NC, EXPERTS, groups, ROWS, width), BF16),
            pltpu.VMEM((EXPERTS, 8, 256), F32),
            pltpu.VMEM((16, 8, 256), F32),
            dma((2,)), dma((NC, 2)), dma((groups,)), dma((groups,)), dma((NC + 1,)), dma((2,)), dma((2,)),
            dma((NC + 1, 3)), dma((NC + 1, 3)), dma((NC + 1, 3)), dma((NC + 1, 3)), dma((NC, 4)), dma((NC, 4)),
        ],
        compiler_params=pltpu.CompilerParams(
            collective_id=0, has_side_effects=True, vmem_limit_bytes=67043328
        ),
        cost_estimate=pl.CostEstimate(
            flops=2 * groups * 256 * depth * hidden, bytes_accessed=200_000_000, transcendentals=0
        ),
    )(tokens, codes, saved, weight)


def place_kernel(grad_ref, out_ref):
    turned = lax.dot_general(
        permutation(), grad_ref[0], (((0,), (0,)), ((), ())), preferred_element_type=F32
    )
    out_ref[0] = turned.astype(BF16)


def place_call(grad):
    groups, rows, hidden = grad.shape
    spec = pl.BlockSpec((1, rows, hidden), lambda g: (g, 0, 0))
    return pl.pallas_call(
        place_kernel,
        name="place",
        grid=(groups,),
        out_shape=jax.ShapeDtypeStruct(grad.shape, BF16),
        in_specs=[spec],
        out_specs=spec,
    )(grad)


def passed_along(value):
    count = lax.axis_size("section")
    return lax.ppermute(value, "section", [(source, source - 1) for source in range(1, count)])


def local(upstream_dy, gate_logits, expert_ids, saved_hidden, down_weight, router_weight):
    highest = lax.Precision.HIGHEST
    micro, per, depth = upstream_dy.shape[1:]
    hidden = down_weight.shape[1]
    logits, chosen, out_grad = gate_logits[0], expert_ids[0], upstream_dy[0]
    gate_prob = jax.nn.sigmoid(logits - logits[..., ::-1])
    onehot = (chosen[..., None] == jnp.arange(EXPERTS, dtype=jnp.int32)).astype(F32)
    picked = jnp.sum(onehot, axis=2)
    earlier = (jnp.arange(per)[:, None] > jnp.arange(per)[None, :]).astype(F32)
    slot = jnp.einsum("ts,mse->mte", earlier, picked) + (jnp.arange(micro) * CAP).astype(F32)[:, None, None]
    gate = jnp.sum(onehot * gate_prob[..., None], axis=2)
    core = lax.rem(lax.axis_index("expert"), SRC).astype(F32)
    base = jnp.floor(slot / 8)
    code = jnp.where(picked > 0, base * 16 + core * 8 + (slot - base * 8), -1.0)
    flat = micro * per
    codes = jnp.concatenate(
        [code.reshape(flat, EXPERTS).T, gate.astype(BF16).astype(F32).reshape(flat, EXPERTS).T]
    )
    saved = saved_hidden[0].transpose(0, 2, 1, 3).reshape(micro * CAP // 8, 256, hidden)
    next_grad = passed_along(out_grad)
    next_router = passed_along(router_weight[0])
    grad, part = expert_call(out_grad.reshape(flat, depth), codes, saved, down_weight[0])
    part = part[:, : micro * CAP * SRC].reshape(NZ, NX, micro * CAP // 8, SRC, 8)
    part = part.transpose(1, 0, 3, 2, 4).reshape(NX * NZ * SRC, micro * CAP)
    returned = lax.all_to_all(part, "expert", split_axis=0, concat_axis=0, tiled=True)
    per_expert = jnp.sum(returned.reshape(EXPERTS, NZ * SRC, micro * CAP), axis=1)
    slots = jnp.arange(micro * CAP).astype(F32)
    select = picked[..., None] * (slot[..., None] == slots).astype(F32)
    token_part = jnp.einsum("mtec,ec->mte", select, per_expert, precision=highest)
    pair_part = jnp.sum(onehot * token_part[:, :, None, :], axis=-1)
    mixed = jnp.sum(gate_prob * pair_part, axis=-1, keepdims=True)
    logit_grad = gate_prob * (pair_part - mixed)
    spread = jnp.sum(onehot * logit_grad[..., None], axis=2)
    spread = passed_along(spread)
    router_term = jnp.einsum("mte,de->mtd", spread, next_router, precision=highest)
    upstream = (next_grad.astype(F32) + router_term).astype(BF16)
    hidden_grad = place_call(grad).reshape(micro, CAP, NX * NZ * SRC, hidden).transpose(0, 2, 1, 3)
    return (hidden_grad[None], upstream[None])


def solution(mesh):
    placed = (
        P("section", None, "expert", None),
        P("section", None, "expert", None),
        P("section", None, "expert", None),
        P("section", None, None, None, "expert"),
        P("section", "expert", None),
        P("section", None, None),
    )
    return jax.shard_map(
        local,
        mesh=mesh,
        in_specs=placed,
        out_specs=(P("section", None, None, None, "expert"), P("section", None, "expert", None)),
        check_vma=False,
    )
```

time: 624 us -> 201 us (0.32)
  waiting for transfers between devices: 424 us -> 3.5 us
  Pallas kernels: 0 us -> 168 us
  starting transfers between devices: 106 us -> 9.22 us
  matrix products: 61.2 us -> 6.39 us
  local copies, waits for them, and re-layouts: 26.7 us -> 5.12 us
    all_to_all x6 -> x1, waiting for transfers between devices: 420 us -> 3.5 us  [local(): lax.all_to_all(part, 'expert', split_axis=0, concat_axis=0, tiled=True)]
    pallas_call x0 -> x2, Pallas kernels: none -> 168 us  [the longest x1 160 us: expert_call(): pl.pallas_call(functools.partial(expert_kernel, groups, width), name='exp...]
    all_to_all x6 -> x1, starting transfers between devices: 105 us -> 5.18 us  [local(): lax.all_to_all(part, 'expert', split_axis=0, concat_axis=0, tiled=True)]
    dot_general x10 -> x3, matrix products: 61.2 us -> 6.39 us  [the longest x1 4.97 us: local(): jnp.einsum('mte,de->mtd', spread, next_router, precision=highest)]
    broadcast_in_dim x2 -> x0, local copies, waits for them, and re-layouts: 11.5 us -> none  [local(): jnp.repeat(routing[0], groups, axis=0)]
    unnamed x12 -> x4, local copies, waits for them, and re-layouts: 8.25 us -> 1.07 us
  transfers between devices with their start and end apart: 7 -> 4, of which waited for: 6 -> 1; matrix products, arithmetic and copies ran while one was open for 11% -> 5% of each run, Pallas kernels for 0% -> 85%
where the time goes in v1:
time: 201 us; the launch traced here: 199 us
  Pallas kernels  168 us (84%)
  starting transfers between devices  9.22 us (5%)
  matrix products  6.39 us (3%)
  other arithmetic  5.14 us (3%)
  local copies, waits for them, and re-layouts  5.12 us (3%)
  waiting for transfers between devices  3.5 us (2%)
    pallas_call x1, Pallas kernels, expert_call(): pl.pallas_call(functools.partial(expert_kernel, groups, width), name='exp...  160 us
    pallas_call x1, Pallas kernels, place_call(): pl.pallas_call(place_kernel, name='place', grid=(groups,), out_shape=jax....  8.79 us
    all_to_all x1, starting transfers between devices, local(): lax.all_to_all(part, 'expert', split_axis=0, concat_axis=0, tiled=True)  5.18 us
    dot_general x1, matrix products, local(): jnp.einsum('mte,de->mtd', spread, next_router, precision=highest)  4.97 us
    ppermute x3, starting transfers between devices, passed_along(): lax.ppermute(value, 'section', [(source, source - 1) for source in range(...  4.04 us
  transfers between devices with their start and end apart: 4, of which 1 were waited for; matrix products, arithmetic and copies ran while one was open for 5% of the time, Pallas kernels for 85%

profile of v1, /device:TPU:1, one launch (start us, length us, event | category | flops | bytes accessed | tf_op | source)
XLA Modules:
  0.0 198.5 jit_solution(12872695575198962361)
XLA Ops:
  0.6 1.3 collective-permute-start
  1.9 0.7 rev.3
  2.7 0.7 add_divide_fusion
  3.3 0.0 copy-start
  3.3 0.6 copy-done
  3.9 0.7 convert_reduce_fusion
  4.6 0.0 copy-start.1
  4.6 0.1 reshape.50
  4.7 0.5 copy-done.1
  5.2 0.7 add_select_fusion
  5.9 0.1 reshape.45
  6.0 0.6 pad_maximum_fusion.ct_hbm
  6.6 159.6 %experts.1 = (bf16[9,256,1024]{2,1,0:T(8,128)(2,1)}, f32[16,256]{1,0:T(8,128)}) custom-call(bf16[128,6144]{1,0:T(8,128)(2,1)} %bitcast.69, f32[8,128]{1,0:T(8,128)} %pad_maximum_fusion.ct_hbm, bf16[9,256,1024]{2,1,0:T(8,128)(2,1)} %bitcast.67, bf16[1024,6144]{1,0:T(8,128)(2,1)} %bitcast.66), custom_call_target="tpu_custom_call" | custom-call | flops 28991029248 | bytes 200000000 | tf_op jit(solution)/shard_map/experts/pallas_call | solution.py:263
  166.2 0.9 reshape.48
  167.1 0.7 all_to_all.6
  167.9 5.2 %all-to-all-start = ((f32[32,1,72]{2,1,0:T(1,128)}), f32[32,1,72]{2,1,0:T(1,128)S(1)}, u32[]{:S(2)}, u32[]{:S(2)}) async-start(f32[32,1,72]{2,1,0:T(1,128)} %bitcast.16), calls=%async_computation | async-start | bytes 32768 | tf_op jit(solution)/shard_map/all_to_all | solution.py:344
  173.0 1.5 collective-permute-start.2
  174.5 0.8 copy.34
  175.3 0.8 copy.33
  176.1 0.3 compare_select_fusion
  176.4 3.5 %all-to-all-done = f32[32,1,72]{2,1,0:T(1,128)S(1)} async-done(((f32[32,1,72]{2,1,0:T(1,128)}), f32[32,1,72]{2,1,0:T(1,128)S(1)}, u32[]{:S(2)}, u32[]{:S(2)}) %all-to-all-start) | async-done | bytes 9248 | tf_op jit(solution)/shard_map/all_to_all | solution.py:344
  180.0 0.7 fusion.2
  180.7 0.7 select_reduce_fusion.1
  181.4 0.7 multiply_reduce_fusion
  182.1 0.7 subtract_multiply_fusion
  182.8 0.7 select_reduce_fusion
  183.4 1.3 collective-permute-start.1
  184.7 8.8 %place.1 = bf16[9,256,1024]{2,1,0:T(8,128)(2,1)} custom-call(bf16[9,256,1024]{2,1,0:T(8,128)(2,1)} %get-tuple-element.4.grad_ref), custom_call_target="tpu_custom_call" | custom-call | tf_op jit(solution)/shard_map/place/pallas_call | solution.py:305
  193.5 0.0 collective-permute-done.1
  193.5 0.0 collective-permute-done.2
  193.5 0.0 collective-permute-done
  193.5 5.0 %fusion = bf16[1,2,64,6144]{3,2,1,0:T(8,128)(2,1)} fusion(bf16[2,64,6144]{2,1,0:T(8,128)(2,1)} %collective-permute-done, f32[2,64,4]{1,2,0:T(4,128)S(1)} %collective-permute-done.1, f32[6144,4]{0,1:T(4,128)S(1)} %collective-permute-done.2), kind=kOutput, calls=%fused_computation.1 | convolution fusion | flops 40108032 | bytes 3246080 | tf_op jit(solution)/shard_map/mte,de->mtd/dot_general | solution.py:354
  (7 shorter events, 0.1 us)
Async XLA Ops:
  0.6 192.9 %collective-permute-start = (bf16[2,64,6144]{2,1,0:T(8,128)(2,1)}, bf16[2,64,6144]{2,1,0:T(8,128)(2,1)}, u32[]{:S(2)}, u32[]{:S(2)}) collective-permute-start(bf16[2,64,6144]{2,1,0:T(8,128)(2,1)} %bitcast.68), channel_id=1, source_target_pairs={{32,0},{64,32},{96,64},{33,1},{65,33},{97,65},{34,2},{66,34},{98,6... | collective-permute-start | bytes 4718600 | tf_op jit(solution)/shard_map/ppermute | solution.py:317
  3.3 0.6 copy-start
  4.6 0.6 copy-start.1
  167.9 12.1 %all-to-all-start = ((f32[32,1,72]{2,1,0:T(1,128)}), f32[32,1,72]{2,1,0:T(1,128)S(1)}, u32[]{:S(2)}, u32[]{:S(2)}) async-start(f32[32,1,72]{2,1,0:T(1,128)} %bitcast.16), calls=%async_computation | async-start | bytes 32768 | tf_op jit(solution)/shard_map/all_to_all | solution.py:344
  173.0 20.5 %collective-permute-start.2 = (f32[6144,4]{0,1:T(4,128)}, f32[6144,4]{0,1:T(4,128)S(1)}, u32[]{:S(2)}, u32[]{:S(2)}) collective-permute-start(f32[6144,4]{0,1:T(4,128)} %bitcast.70), channel_id=1, source_target_pairs={{32,0},{64,32},{96,64},{33,1},{65,33},{97,65},{34,2},{66,34},{98,6... | collective-permute-start | bytes 294920 | tf_op jit(solution)/shard_map/ppermute | solution.py:317
  183.4 10.1 %collective-permute-start.1 = (f32[2,64,4]{1,2,0:T(4,128)S(1)}, f32[2,64,4]{1,2,0:T(4,128)S(1)}, u32[]{:S(2)}, u32[]{:S(2)}) collective-permute-start(f32[2,64,4]{1,2,0:T(4,128)S(1)} %select_reduce_fusion), channel_id=1, source_target_pairs={{32,0},{64,32},{96,64},{33,1},{65,33},{97,65},{34,2},{66,34},{98,6... | collective-permute-start | bytes 6152 | tf_op jit(solution)/shard_map/ppermute | solution.py:317

commit v2 on v0

v2 whole, which is shorter than its diff:
```python
import functools

import jax
import jax.numpy as jnp
from jax import lax
from jax.experimental import pallas as pl
from jax.experimental.pallas import tpu as pltpu
from jax.sharding import PartitionSpec as P

EXPERTS = 4
CAP = 36
NX = 4
NZ = 4
NC = 12
A_CHUNKS = (0, 1, 2, 3, 4, 5, 6)
B_CHUNKS = (7, 8, 9, 10, 11)
ORDER = ((0, 7), (1, 8), (2, 3), (9, 4), (10,), (5,), (11,), (6,))
ROWS = 16
MESH = pl.DeviceIdType.MESH
F32 = jnp.float32
BF16 = jnp.bfloat16
NT = (((1,), (1,)), ((), ()))
HIGHEST = lax.Precision.HIGHEST


def permutation(turned):
    i = lax.broadcasted_iota(jnp.int32, (256, 256), 1 if turned else 0)
    n = lax.broadcasted_iota(jnp.int32, (256, 256), 0 if turned else 1)
    z, x, src, slot = i >> 6, (i >> 4) & 3, (i >> 3) & 1, i & 7
    return (n == slot * 32 + (x * 4 + z) * 2 + src).astype(F32).astype(BF16)


def codes_of(tile, src):
    picks = [(tile[0:1] == e).astype(F32) for e in range(EXPERTS)], [(tile[1:2] == e).astype(F32) for e in range(EXPERTS)]
    picked = jnp.concatenate([a + b for a, b in zip(*picks)] * 2, axis=0)
    t = lax.broadcasted_iota(jnp.int32, (128, 128), 0)
    u = lax.broadcasted_iota(jnp.int32, (128, 128), 1)
    earlier = ((t < u) & ((t >> 6) == (u >> 6))).astype(F32).astype(BF16)
    rank = jnp.dot(picked.astype(BF16), earlier, preferred_element_type=F32)
    micro = (lax.broadcasted_iota(jnp.int32, (8, 128), 1) >> 6).astype(F32)
    slot = rank + micro * CAP
    base = jnp.floor(slot * 0.125)
    code = jnp.where(picked > 0, base * 8 + slot + src * 8, -1.0)
    diff = tile[2:3] - tile[3:4]
    first, second = jax.nn.sigmoid(diff), jax.nn.sigmoid(-diff)
    gate = jnp.concatenate([a * first + b * second for a, b in zip(*picks)] * 2, axis=0)
    return code, gate


def expert_kernel(
    groups, width, x_hbm, info_hbm, saved_hbm, w_hbm, router_hbm, grad_hbm, next_hbm, nrouter_hbm, spread_ref,
    rows, wv, acc, sv, x2, info, selz, packed, raw_z, packed_z, gs, gt, own_gate, pts, pr, sums, spread,
    x_sem, w_sem, s_sem, o_sem, loc_sem, b0_send, b0_recv, xs, xr, zs, zr, bs, br, ps, pr_sem,
):
    me = lax.axis_index("expert")
    section = lax.axis_index("section")
    mx, mz, mc = me // 8, (me // 2) % 4, me % 2
    half = width * NC

    def dev(x, z, c, s=0):
        index = (lax.rem(x + 8, NX) * NZ + lax.rem(z + 8, NZ)) * 2 + c
        return (lax.rem(section + s + 4, 4), index)

    sibling = dev(mx, mz, 1 - mc)
    xdev = [dev(mx + d, mz, mc) for d in range(NX)]
    zdev = [dev(mx, mz + d, mc) for d in range(NZ)]
    before, after = dev(mx, mz, mc, -1), dev(mx, mz, mc, 1)
    chips = [(dx, dz) for dx in range(NX) for dz in range(NZ) if dx or dz]

    barrier = pltpu.get_barrier_semaphore()
    partners = [sibling, before, after] + [dev(mx + dx, mz + dz, mc) for dx, dz in chips]
    for target in partners:
        pl.semaphore_signal(barrier, inc=1, device_id=target, device_id_type=MESH)
    pl.semaphore_wait(barrier, len(partners))

    def remote(src, dst, send, recv, target):
        return pltpu.make_async_remote_copy(
            src_ref=src, dst_ref=dst, send_sem=send, recv_sem=recv, device_id=target, device_id_type=MESH
        )

    waits = []

    def send(src, dst, send_sem, recv_sem, target):
        copy = remote(src, dst, send_sem, recv_sem, target)
        copy.start()
        waits.append(copy)

    def arrived(ref, sem):
        remote(ref, ref, b0_send.at[0], sem, sibling).wait_recv()

    mine = pl.ds(pl.multiple_of(mc * half, 128), half)
    other = pl.ds(pl.multiple_of((1 - mc) * half, 128), half)
    mine_rows = pl.ds(pl.multiple_of(mc * 128, 128), 128)
    sib_rows = pl.ds(pl.multiple_of((1 - mc) * 128, 128), 128)
    send(info_hbm, info.at[mz, mc], b0_send.at[1], b0_recv.at[1], sibling)
    send(x_hbm.at[:, other], x2.at[mine_rows, :], b0_send.at[0], b0_recv.at[0], sibling)
    own_x = pltpu.make_async_copy(x_hbm.at[:, mine], x2.at[mine_rows, :], x_sem.at[0])
    own_c = pltpu.make_async_copy(info_hbm, info.at[mz, mc], x_sem.at[1])
    own_c.start()
    own_x.start()

    order = [k for ks in ORDER for k in ks]

    def w_copies(i):
        copies = []
        for n, k in enumerate(ORDER[i]):
            for h in range(2):
                cols = pl.ds(h * half + k * width, width)
                copies.append(
                    pltpu.make_async_copy(w_hbm.at[:, cols], wv.at[i % 2, n * 2 + h], w_sem.at[i % 2, n * 2 + h])
                )
        return copies

    for i in range(2):
        for copy in w_copies(i):
            copy.start()
    s_copy = [pltpu.make_async_copy(saved_hbm.at[g], sv.at[g], s_sem.at[g]) for g in range(groups)]
    for copy in s_copy:
        copy.start()
    send(x_hbm, next_hbm, b0_send.at[2], b0_recv.at[2], before)
    send(router_hbm, nrouter_hbm, b0_send.at[3], b0_recv.at[3], before)

    def select(z):
        code0, gate0 = codes_of(info[z, 0], 0)
        code1, gate1 = codes_of(info[z, 1], 1)
        row = lax.broadcasted_iota(jnp.int32, (groups * ROWS, 256), 0).astype(F32)
        gates = []
        for e in range(EXPERTS):
            code = jnp.concatenate([code0[e : e + 1], code1[e : e + 1]], axis=1)
            selz[z, e] = (row == code).astype(F32).astype(BF16)
            gates.append(jnp.concatenate([gate0[e : e + 1], gate1[e : e + 1]], axis=1))
        return gates, gate0, gate1

    gs[...] = jnp.zeros_like(gs)
    own_c.wait()
    arrived(info.at[mz, 1 - mc], b0_recv.at[1])
    for d in (1, 3, 2):
        send(info.at[mz], info.at[mz], zs.at[NC + 1, d - 1], zr.at[NC + 1, d - 1], zdev[d])
    gates, gate0, gate1 = select(mz)
    own_gate[...] = jnp.where(mc == 0, gate0, gate1)
    for e in range(EXPERTS):
        gs[e, :, 0 : groups * ROWS] = lax.dot_general(
            jnp.broadcast_to(gates[e], (8, 256)).astype(BF16), selz[mz, e], NT, preferred_element_type=F32
        )
    own_x.wait()
    arrived(x2.at[sib_rows, :], b0_recv.at[0])

    def columns(k):
        return slice(k * width, (k + 1) * width)

    def start_raw(k):
        b = B_CHUNKS.index(k)
        for d in (1, 3, 2):
            send(x2.at[:, columns(k)], raw_z.at[b, mz], zs.at[k, d - 1], zr.at[k, d - 1], zdev[d])

    def pack(k):
        a = A_CHUNKS.index(k)
        for e in range(EXPERTS):
            block = jnp.dot(selz[mz, e], x2[:, columns(k)], preferred_element_type=F32)
            packed[a, e] = block.astype(BF16).reshape(groups, ROWS, width)

    locals_ = {}

    def start_x(k):
        if k == NC:
            here = gs.at
            there = gt.at[mz, mx]
        elif k in A_CHUNKS:
            here = packed.at[A_CHUNKS.index(k)].at
            there = rows.at[k, mc, :, mz, mx]
        else:
            here = packed_z.at[B_CHUNKS.index(k)].at
            there = rows.at[k, mc, :, :, mx]
        locals_[k] = pltpu.make_async_copy(here[mx], there, loc_sem.at[k])
        locals_[k].start()
        for d in (2, 1, 3):
            send(here[lax.rem(mx + d, NX)], there, xs.at[k, d - 1], xr.at[k, d - 1], xdev[d])

    def wait_x(k):
        locals_[k].wait()
        for d in (1, 2, 3):
            x = lax.rem(mx - d + NX, NX)
            if k == NC:
                ref = gt.at[mz, x]
            elif k in A_CHUNKS:
                ref = rows.at[k, mc, :, mz, x]
            else:
                ref = rows.at[k, mc, :, :, x]
            arrived(ref, xr.at[k, d - 1])

    def around_z(k):
        wait_x(k)
        ref = gt.at[mz] if k == NC else rows.at[k, mc, :, mz]
        for d in (1, 3, 2):
            send(ref, ref, zs.at[k, d - 1], zr.at[k, d - 1], zdev[d])
        if k < NC:
            send(ref, ref, bs.at[k, 0], br.at[k, 0], sibling)

    def cross_x(k):
        b = B_CHUNKS.index(k)
        for d in range(NZ):
            z = lax.rem(mz + d, NZ)
            if d:
                arrived(raw_z.at[b, z], zr.at[k, NZ - d - 1])
            tokens = raw_z[b, z] if d else x2[:, columns(k)]
            for e in range(EXPERTS):
                block = jnp.dot(selz[z, e], tokens, preferred_element_type=F32)
                packed_z[b, e, :, z] = block.astype(BF16).reshape(groups, ROWS, width)
        start_x(k)

    def take(k):
        if k in A_CHUNKS:
            for d in (1, 3, 2):
                ref = rows.at[k, mc, :, lax.rem(mz - d + NZ, NZ)]
                arrived(ref, zr.at[k, d - 1])
                send(ref, ref, bs.at[k, d], br.at[k, d], sibling)
        else:
            wait_x(k)
            send(rows.at[k, mc], rows.at[k, mc], bs.at[k, 0], br.at[k, 0], sibling)

    def shared(k):
        if k in A_CHUNKS:
            for d in range(NZ):
                arrived(rows.at[k, 1 - mc, :, lax.rem(mz - d + NZ, NZ)], br.at[k, d])
        else:
            arrived(rows.at[k, 1 - mc], br.at[k, 0])

    big = groups // 3

    def compute(i):
        for k in ORDER[i]:
            shared(k)
        for copy in w_copies(i):
            copy.wait()

        def body(m, carry):
            at = pl.ds(m * big, big)
            total = None
            for n, k in enumerate(ORDER[i]):
                for h in range(2):
                    left = rows[k, h, at].reshape(big * 256, width)
                    term = lax.dot_general(left, wv[i % 2, n * 2 + h], NT, preferred_element_type=F32)
                    total = term if total is None else total + term
            total = total.reshape(big, 256, total.shape[-1])
            acc[at] = total if i == 0 else acc[at] + total
            return carry

        lax.fori_loop(0, 3, body, 0)
        if i + 2 < len(ORDER):
            for copy in w_copies(i + 2):
                copy.start()

    start_x(NC)
    for n, k in enumerate(A_CHUNKS):
        pack(k)
        if n:
            start_x(A_CHUNKS[n - 1])
        if n < len(B_CHUNKS):
            start_raw(B_CHUNKS[n])
    start_x(A_CHUNKS[-1])
    around_z(NC)
    for d in (1, 2, 3):
        z = lax.rem(mz + d, NZ)
        arrived(info.at[z], zr.at[NC + 1, NZ - d - 1])
        select(z)
    for n, k in enumerate(A_CHUNKS):
        around_z(k)
        if n < len(B_CHUNKS):
            cross_x(B_CHUNKS[n])
    perm = permutation(False)

    def place_saved(g, carry):
        sv[g] = jnp.dot(perm, sv[g], preferred_element_type=F32).astype(BF16)
        return carry

    for copy in s_copy:
        copy.wait()
    lax.fori_loop(0, groups, place_saved, 0)
    for d in (1, 2, 3):
        arrived(gt.at[lax.rem(mz - d + NZ, NZ)], zr.at[NC, d - 1])
    for i, ks in enumerate(ORDER):
        for k in ks:
            take(k)
        if i:
            compute(i - 1)
    compute(len(ORDER) - 1)

    lane = lax.broadcasted_iota(jnp.int32, (256, 256), 1)
    row16 = lax.broadcasted_iota(jnp.int32, (256, 256), 0) & 15

    def dots(g, total):
        raw = acc[g]
        part = jnp.sum(raw * sv[g].astype(F32), axis=1, keepdims=True)
        part = jnp.where(lane == row16 + g * 16, part, 0.0).reshape(16, 16, 256)
        return total + jnp.sum(part, axis=1)

    part = lax.fori_loop(0, groups, dots, jnp.zeros((16, 256), F32))
    pts[...] = jnp.broadcast_to(part[:, None, :], (16, 8, 256))
    slot = mx * NZ + mz
    own_part = pltpu.make_async_copy(pts.at[mz * NX + mx], pr.at[slot], loc_sem.at[NC + 1])
    own_part.start()
    for n, (dx, dz) in enumerate(chips):
        x, z = lax.rem(mx + dx, NX), lax.rem(mz + dz, NZ)
        send(pts.at[z * NX + x], pr.at[slot], ps.at[n], pr_sem.at[n], dev(x, z, mc))

    gates = jnp.broadcast_to(gt[...].reshape(16, 8, 256)[:, 0:1, :], (16, 16, 256)).reshape(256, 256)

    def finish(g, carry):
        gate = jnp.sum(jnp.where(lane == row16 + g * 16, gates, 0.0), axis=1, keepdims=True)
        sv[g] = (gate * acc[g]).astype(BF16)
        pltpu.make_async_copy(sv.at[g], grad_hbm.at[g], o_sem.at[g]).start()
        return carry

    lax.fori_loop(0, groups, finish, 0)

    own_part.wait()
    for n, (dx, dz) in enumerate(chips):
        x, z = lax.rem(mx - dx + NX, NX), lax.rem(mz - dz + NZ, NZ)
        arrived(pr.at[x * NZ + z], pr_sem.at[n])
    summed = jnp.sum(pr[...].reshape(EXPERTS, NZ, 8, 256), axis=1)
    sums[0] = summed
    send(sums.at[0], sums.at[1], bs.at[NC, 0], br.at[NC, 0], sibling)
    arrived(sums.at[1], br.at[NC, 0])
    summed = summed + sums[1]
    token = []
    for e in range(EXPERTS):
        chosen = jnp.where(mc == 0, selz[mz, e, :, 0:128].astype(F32), selz[mz, e, :, 128:256].astype(F32))
        token.append(
            jnp.dot(summed[e, :, 0 : groups * ROWS], chosen, preferred_element_type=F32, precision=HIGHEST)[0:1]
        )
    token = jnp.concatenate(token * 2, axis=0)
    gate = own_gate[...]
    mixed = jnp.sum((gate * token)[0:EXPERTS], axis=0, keepdims=True)
    spread[0] = gate * (token - mixed)
    send(spread.at[0], spread.at[1], b0_send.at[4], b0_recv.at[4], before)
    for g in range(groups):
        pltpu.make_async_copy(sv.at[g], grad_hbm.at[g], o_sem.at[g]).wait()
    arrived(next_hbm, b0_recv.at[2])
    arrived(nrouter_hbm, b0_recv.at[3])
    arrived(spread.at[1], b0_recv.at[4])
    spread_ref[...] = spread[1]
    for copy in waits:
        copy.wait_send()


def expert_call(tokens, info, saved, weight, router):
    depth, hidden = tokens.shape[-1], weight.shape[0]
    groups = saved.shape[0]
    width = depth // 2 // NC
    dma = pltpu.SemaphoreType.DMA
    anywhere = pl.BlockSpec(memory_space=pl.ANY)
    na, nb = len(A_CHUNKS), len(B_CHUNKS)
    return pl.pallas_call(
        functools.partial(expert_kernel, groups, width),
        name="experts",
        out_shape=(
            jax.ShapeDtypeStruct((groups, 256, hidden), BF16),
            jax.ShapeDtypeStruct(tokens.shape, BF16),
            jax.ShapeDtypeStruct(router.shape, F32),
            jax.ShapeDtypeStruct((8, 128), F32),
        ),
        in_specs=[anywhere] * 5,
        out_specs=(anywhere, anywhere, anywhere, pl.BlockSpec(memory_space=pltpu.VMEM)),
        scratch_shapes=[
            pltpu.VMEM((NC, 2, groups, NZ, NX, ROWS, width), BF16),
            pltpu.VMEM((2, 4, hidden, width), BF16),
            pltpu.VMEM((groups, 256, hidden), F32),
            pltpu.VMEM((groups, 256, hidden), BF16),
            pltpu.VMEM((256, depth // 2), BF16),
            pltpu.VMEM((NZ, 2, 8, 128), F32),
            pltpu.VMEM((NZ, EXPERTS, groups * ROWS, 256), BF16),
            pltpu.VMEM((na, EXPERTS, groups, ROWS, width), BF16),
            pltpu.VMEM((nb, NZ, 256, width), BF16),
            pltpu.VMEM((nb, EXPERTS, groups, NZ, ROWS, width), BF16),
            pltpu.VMEM((EXPERTS, 8, 256), F32),
            pltpu.VMEM((NZ, NX, 8, 256), F32),
            pltpu.VMEM((8, 128), F32),
            pltpu.VMEM((16, 8, 256), F32),
            pltpu.VMEM((16, 8, 256), F32),
            pltpu.VMEM((2, EXPERTS, 8, 256), F32),
            pltpu.VMEM((2, 8, 128), F32),
            dma((2,)), dma((2, 4)), dma((groups,)), dma((groups,)), dma((NC + 2,)), dma((5,)), dma((5,)),
            dma((NC + 1, 3)), dma((NC + 1, 3)), dma((NC + 2, 3)), dma((NC + 2, 3)), dma((NC + 1, 4)), dma((NC + 1, 4)),
            dma((15,)), dma((15,)),
        ],
        compiler_params=pltpu.CompilerParams(
            collective_id=0, has_side_effects=True, vmem_limit_bytes=67043328
        ),
        cost_estimate=pl.CostEstimate(
            flops=2 * groups * 256 * depth * hidden, bytes_accessed=200_000_000, transcendentals=0
        ),
    )(tokens, info, saved, weight, router)


def last_kernel(grad_ref, tokens_ref, router_ref, spread_ref, hidden_ref, upstream_ref, perm):
    @pl.when(pl.program_id(0) == 0)
    def _():
        perm[...] = permutation(True)

    for g in range(grad_ref.shape[0]):
        hidden_ref[g] = jnp.dot(perm[...], grad_ref[g], preferred_element_type=F32).astype(BF16)
    live = lax.axis_index("section") < lax.axis_size("section") - 1
    spread = jnp.transpose(spread_ref[...])
    total = tokens_ref[...].astype(F32)
    for e in range(EXPERTS):
        total = total + spread[:, e : e + 1] * router_ref[e : e + 1, :]
    upstream_ref[...] = jnp.where(live, total, 0.0).astype(BF16)


def last_call(grad, tokens, router, spread):
    groups, rows, hidden = grad.shape
    flat, depth = tokens.shape
    steps = 3
    grad_spec = pl.BlockSpec((groups // steps, rows, hidden), lambda s: (s, 0, 0))
    token_spec = pl.BlockSpec((flat, depth // steps), lambda s: (0, s))
    return pl.pallas_call(
        last_kernel,
        name="last",
        grid=(steps,),
        out_shape=(jax.ShapeDtypeStruct(grad.shape, BF16), jax.ShapeDtypeStruct(tokens.shape, BF16)),
        in_specs=[
            grad_spec,
            token_spec,
            pl.BlockSpec((EXPERTS, depth // steps), lambda s: (0, s)),
            pl.BlockSpec((8, 128), lambda s: (0, 0)),
        ],
        out_specs=(grad_spec, token_spec),
        scratch_shapes=[pltpu.VMEM((256, 256), BF16)],
    )(grad, tokens, router, spread)


def local(upstream_dy, gate_logits, expert_ids, saved_hidden, down_weight, router_weight):
    micro, per, depth = upstream_dy.shape[1:]
    hidden = down_weight.shape[1]
    flat = micro * per
    info = jnp.concatenate(
        [
            expert_ids[0].transpose(2, 0, 1).reshape(2, flat).astype(F32),
            gate_logits[0].transpose(2, 0, 1).reshape(2, flat),
            jnp.zeros((4, flat), F32),
        ]
    )
    saved = saved_hidden[0].transpose(0, 2, 1, 3).reshape(micro * CAP // 8, 256, hidden)
    grad, tokens, router, spread = expert_call(
        upstream_dy[0].reshape(flat, depth), info, saved, down_weight[0], router_weight[0].T
    )
    hidden_grad, upstream = last_call(grad, tokens, router, spread)
    hidden_grad = hidden_grad.reshape(micro, CAP, NX * NZ * 2, hidden).transpose(0, 2, 1, 3)
    return (hidden_grad[None], upstream.reshape(micro, per, depth)[None])


def solution(mesh):
    placed = (
        P("section", None, "expert", None),
        P("section", None, "expert", None),
        P("section", None, "expert", None),
        P("section", None, None, None, "expert"),
        P("section", "expert", None),
        P("section", None, None),
    )
    return jax.shard_map(
        local,
        mesh=mesh,
        in_specs=placed,
        out_specs=(P("section", None, None, None, "expert"), P("section", None, "expert", None)),
        check_vma=False,
    )
```

time: 624 us -> 163 us (0.26)
  waiting for transfers between devices: 424 us -> 0 us
  Pallas kernels: 0 us -> 160 us
  starting transfers between devices: 106 us -> 0 us
  matrix products: 61.2 us -> 0 us
  local copies, waits for them, and re-layouts: 26.7 us -> 0.93 us
    all_to_all x6 -> x0, waiting for transfers between devices: 420 us -> none  [the longest x2 401 us: local(): lax.all_to_all(jnp.repeat(routing[0], groups, axis=0), 'expert', split_ax...]
    pallas_call x0 -> x2, Pallas kernels: none -> 160 us  [the longest x1 152 us: expert_call(): pl.pallas_call(functools.partial(expert_kernel, groups, width), name='exp...]
    all_to_all x6 -> x0, starting transfers between devices: 105 us -> none  [the longest x2 49.5 us: local(): lax.all_to_all(jnp.repeat(routing[0], groups, axis=0), 'expert', split_ax...]
    dot_general x10 -> x0, matrix products: 61.2 us -> none  [the longest x2 53.4 us: expert_part(): jnp.einsum('rd,hd->rh', flat_rows, weight, preferred_element_type=jnp.flo...]
    broadcast_in_dim x2 -> x1, local copies, waits for them, and re-layouts: 11.5 us -> 0.01 us  [local(): jnp.zeros((4, flat), F32)]
    unnamed x12 -> x0, local copies, waits for them, and re-layouts: 8.25 us -> none
  transfers between devices with their start and end apart: 7 -> 0, of which waited for: 6 -> 0; matrix products, arithmetic and copies ran while one was open for 11% -> 0% of each run, Pallas kernels for 0% -> 0%
where the time goes in v2:
time: 163 us
  Pallas kernels  160 us (98%)
    pallas_call x1, Pallas kernels, expert_call(): pl.pallas_call(functools.partial(expert_kernel, groups, width), name='exp...  152 us
    pallas_call x1, Pallas kernels, last_call(): pl.pallas_call(last_kernel, name='last', grid=(steps,), out_shape=(jax.Sh...  7.67 us

profile of v2, /device:TPU:1, one launch (start us, length us, event | category | flops | bytes accessed | tf_op | source)
XLA Modules:
  0.0 162.7 jit_solution(9894908209344757600)
XLA Ops:
  0.6 0.1 pad.2.clone
  0.7 0.7 copy.9
  1.4 0.1 reshape.16
  1.5 0.7 convert_bitcast_fusion
  2.2 0.1 convert_element_type.15
  2.3 0.7 maximum_maximum_fusion.info_hbm
  2.9 152.1 %experts.1 = (bf16[9,256,1024]{2,1,0:T(8,128)(2,1)}, bf16[128,6144]{1,0:T(8,128)(2,1)}, f32[4,6144]{1,0:T(4,128)}, f32[8,128]{1,0:T(8,128)}) custom-call(bf16[128,6144]{1,0:T(8,128)(2,1)} %bitcast.27, f32[8,128]{1,0:T(8,128)} %maximum_maximum_fusion.info_hbm, bf16[9,256,1024]{2,1,0:T(8,128)(2,1)} %bitcast.25, bf16[1024,6144]{1,0:T(8,128)(2,1)} %bitcast.24, ...), custom_call_target="tpu_custom_call" | custom-call | flops 28991029248 | bytes 200000000 | tf_op jit(solution)/shard_map/experts/pallas_call | solution.py:353
  155.0 7.7 %last.1 = (bf16[9,256,1024]{2,1,0:T(8,128)(2,1)}, bf16[128,6144]{1,0:T(8,128)(2,1)}) custom-call(bf16[9,256,1024]{2,1,0:T(8,128)(2,1)} %get-tuple-element.8.grad_ref, bf16[128,6144]{1,0:T(8,128)(2,1)} %get-tuple-element.9.tokens_ref, f32[4,6144]{1,0:T(4,128)} %get-tuple-element.10.router_ref, f32[8,128]{1,0:T(8,128)} %get-tuple-element.11.spread_ref), custom_call_target="tpu_custom_call" | custom-call | tf_op jit(solution)/shard_map/last/pallas_call | solution.py:416
  (2 shorter events, 0.0 us)

commit v3 on v2

--- a/solution.py
+++ b/solution.py
@@ -12,9 +12,22 @@
 NX = 4
 NZ = 4
 NC = 12
-A_CHUNKS = (0, 1, 2, 3, 4, 5, 6)
-B_CHUNKS = (7, 8, 9, 10, 11)
-ORDER = ((0, 7), (1, 8), (2, 3), (9, 4), (10,), (5,), (11,), (6,))
+A_CHUNKS = (0, 2, 4, 6, 8, 10, 11)
+B_CHUNKS = (1, 3, 5, 7, 9)
+ORDER = ((1, 0), (3, 2), (4, 5), (6, 7), (8,), (10,), (9,), (11,))
+PIECES = 12
+FIRST = (
+    "t1", "g12", "x12", "p0", "p2", "x0", "t3", "t5", "p4", "x2", "t7", "p6",
+    "x4", "p8", "x6", "t9", "p10", "x8", "p11", "x10", "x11",
+)
+EARLY = (
+    "r1", "r3", "a0", "r5", "c1", "r7", "c3", "r9", "a2", "c5", "c7", "c9",
+)
+LATE = (
+    "n0", "a4", "n2", "a6", "w1", "f0", "m0", "n4", "a8", "w3", "f2", "m1",
+    "n6", "a10", "f4", "w5", "n8", "a11", "m2", "f6", "n10", "w7", "m3", "f8",
+    "n11", "m4", "f10", "w9", "m5", "f11", "m6",
+)
 ROWS = 16
 MESH = pl.DeviceIdType.MESH
 F32 = jnp.float32
@@ -30,8 +43,9 @@
     return (n == slot * 32 + (x * 4 + z) * 2 + src).astype(F32).astype(BF16)
 
 
-def codes_of(tile, src):
-    picks = [(tile[0:1] == e).astype(F32) for e in range(EXPERTS)], [(tile[1:2] == e).astype(F32) for e in range(EXPERTS)]
+def codes_of(ids, logits, src):
+    chosen = [jnp.concatenate([ids[0, k : k + 1], ids[1, k : k + 1]], axis=1) for k in range(2)]
+    picks = [[(row == e).astype(F32) for e in range(EXPERTS)] for row in chosen]
     picked = jnp.concatenate([a + b for a, b in zip(*picks)] * 2, axis=0)
     t = lax.broadcasted_iota(jnp.int32, (128, 128), 0)
     u = lax.broadcasted_iota(jnp.int32, (128, 128), 1)
@@ -41,15 +55,18 @@
     slot = rank + micro * CAP
     base = jnp.floor(slot * 0.125)
     code = jnp.where(picked > 0, base * 8 + slot + src * 8, -1.0)
-    diff = tile[2:3] - tile[3:4]
+    if logits is None:
+        return code, None
+    logit = [jnp.concatenate([logits[0, k : k + 1], logits[1, k : k + 1]], axis=1) for k in range(2)]
+    diff = logit[0] - logit[1]
     first, second = jax.nn.sigmoid(diff), jax.nn.sigmoid(-diff)
     gate = jnp.concatenate([a * first + b * second for a, b in zip(*picks)] * 2, axis=0)
     return code, gate
 
 
 def expert_kernel(
-    groups, width, x_hbm, info_hbm, saved_hbm, w_hbm, router_hbm, grad_hbm, next_hbm, nrouter_hbm, spread_ref,
-    rows, wv, acc, sv, x2, info, selz, packed, raw_z, packed_z, gs, gt, own_gate, pts, pr, sums, spread,
+    groups, width, x_hbm, ids_hbm, logits_hbm, saved_hbm, w_hbm, router_hbm, grad_hbm, next_hbm, nrouter_hbm, spread_ref,
+    rows, wv, acc, sv, x2, info, logits, selz, packed, raw_z, packed_z, gs, gt, own_gate, pts, pr, sums, spread,
     x_sem, w_sem, s_sem, o_sem, loc_sem, b0_send, b0_recv, xs, xr, zs, zr, bs, br, ps, pr_sem,
 ):
     me = lax.axis_index("expert")
@@ -67,39 +84,56 @@
     before, after = dev(mx, mz, mc, -1), dev(mx, mz, mc, 1)
     chips = [(dx, dz) for dx in range(NX) for dz in range(NZ) if dx or dz]
 
+    def remote(src, dst, send, recv, target):
+        return pltpu.make_async_remote_copy(
+            src_ref=src, dst_ref=dst, send_sem=send, recv_sem=recv, device_id=target, device_id_type=MESH
+        )
+
+    waits = []
+
+    def send(src, dst, send_sem, recv_sem, target):
+        copy = remote(src, dst, send_sem, recv_sem, target)
+        copy.start()
+        waits.append(copy)
+
+    def arrived(ref, sem):
+        remote(ref, ref, b0_send.at[0], sem, sibling).wait_recv()
+
+    mine_rows = pl.ds(pl.multiple_of(mc * 128, 128), 128)
+    sib_rows = pl.ds(pl.multiple_of((1 - mc) * 128, 128), 128)
+    own_c = pltpu.make_async_copy(ids_hbm, info.at[mz, mc], x_sem.at[PIECES])
+    own_c.start()
+    own_l = pltpu.make_async_copy(logits_hbm, logits.at[mc], x_sem.at[PIECES + 1])
+    own_l.start()
+    piece = half // PIECES
+    own_x = []
+    for q in range(PIECES):
+        cols = pl.ds(pl.multiple_of(mc * half + q * piece, 128), piece)
+        own_x.append(
+            pltpu.make_async_copy(x_hbm.at[:, cols], x2.at[mine_rows, q * piece : (q + 1) * piece], x_sem.at[q])
+        )
+        own_x[q].start()
+
     barrier = pltpu.get_barrier_semaphore()
     partners = [sibling, before, after] + [dev(mx + dx, mz + dz, mc) for dx, dz in chips]
     for target in partners:
         pl.semaphore_signal(barrier, inc=1, device_id=target, device_id_type=MESH)
     pl.semaphore_wait(barrier, len(partners))
 
-    def remote(src, dst, send, recv, target):
-        return pltpu.make_async_remote_copy(
-            src_ref=src, dst_ref=dst, send_sem=send, recv_sem=recv, device_id=target, device_id_type=MESH
-        )
-
-    waits = []
-
-    def send(src, dst, send_sem, recv_sem, target):
-        copy = remote(src, dst, send_sem, recv_sem, target)
-        copy.start()
-        waits.append(copy)
-
-    def arrived(ref, sem):
-        remote(ref, ref, b0_send.at[0], sem, sibling).wait_recv()
-
-    mine = pl.ds(pl.multiple_of(mc * half, 128), half)
-    other = pl.ds(pl.multiple_of((1 - mc) * half, 128), half)
-    mine_rows = pl.ds(pl.multiple_of(mc * 128, 128), 128)
-    sib_rows = pl.ds(pl.multiple_of((1 - mc) * 128, 128), 128)
-    send(info_hbm, info.at[mz, mc], b0_send.at[1], b0_recv.at[1], sibling)
-    send(x_hbm.at[:, other], x2.at[mine_rows, :], b0_send.at[0], b0_recv.at[0], sibling)
-    own_x = pltpu.make_async_copy(x_hbm.at[:, mine], x2.at[mine_rows, :], x_sem.at[0])
-    own_c = pltpu.make_async_copy(info_hbm, info.at[mz, mc], x_sem.at[1])
-    own_c.start()
-    own_x.start()
-
-    order = [k for ks in ORDER for k in ks]
+    send(ids_hbm, info.at[mz, mc], b0_send.at[1], b0_recv.at[1], sibling)
+    send(logits_hbm, logits.at[mc], b0_send.at[0], b0_recv.at[0], sibling)
+    for q in range(PIECES):
+        cols = pl.ds(pl.multiple_of((1 - mc) * half + q * piece, 128), piece)
+        to = x2.at[mine_rows, q * piece : (q + 1) * piece]
+        send(x_hbm.at[:, cols], to, b0_send.at[5 + q], b0_recv.at[5 + q], sibling)
+    swapped = set()
+
+    def swap_done(k):
+        q = k * width // piece
+        if q not in swapped:
+            swapped.add(q)
+            own_x[q].wait()
+            arrived(x2.at[sib_rows, q * piece : (q + 1) * piece], b0_recv.at[5 + q])
 
     def w_copies(i):
         copies = []
@@ -120,41 +154,54 @@
     send(x_hbm, next_hbm, b0_send.at[2], b0_recv.at[2], before)
     send(router_hbm, nrouter_hbm, b0_send.at[3], b0_recv.at[3], before)
 
-    def select(z):
-        code0, gate0 = codes_of(info[z, 0], 0)
-        code1, gate1 = codes_of(info[z, 1], 1)
+    def select(z, own=False):
+        code0, gate0 = codes_of(info[z, 0], logits[0] if own else None, 0)
+        code1, gate1 = codes_of(info[z, 1], logits[1] if own else None, 1)
         row = lax.broadcasted_iota(jnp.int32, (groups * ROWS, 256), 0).astype(F32)
         gates = []
         for e in range(EXPERTS):
             code = jnp.concatenate([code0[e : e + 1], code1[e : e + 1]], axis=1)
             selz[z, e] = (row == code).astype(F32).astype(BF16)
-            gates.append(jnp.concatenate([gate0[e : e + 1], gate1[e : e + 1]], axis=1))
+            if own:
+                gates.append(jnp.concatenate([gate0[e : e + 1], gate1[e : e + 1]], axis=1))
         return gates, gate0, gate1
 
     gs[...] = jnp.zeros_like(gs)
-    own_c.wait()
-    arrived(info.at[mz, 1 - mc], b0_recv.at[1])
-    for d in (1, 3, 2):
-        send(info.at[mz], info.at[mz], zs.at[NC + 1, d - 1], zr.at[NC + 1, d - 1], zdev[d])
-    gates, gate0, gate1 = select(mz)
-    own_gate[...] = jnp.where(mc == 0, gate0, gate1)
-    for e in range(EXPERTS):
-        gs[e, :, 0 : groups * ROWS] = lax.dot_general(
-            jnp.broadcast_to(gates[e], (8, 256)).astype(BF16), selz[mz, e], NT, preferred_element_type=F32
-        )
-    own_x.wait()
-    arrived(x2.at[sib_rows, :], b0_recv.at[0])
+
+    def own_select(_):
+        own_c.wait()
+        own_l.wait()
+        arrived(info.at[mz, 1 - mc], b0_recv.at[1])
+        arrived(logits.at[1 - mc], b0_recv.at[0])
+        for d in (1, 3, 2):
+            send(info.at[mz], info.at[mz], zs.at[NC + 1, d - 1], zr.at[NC + 1, d - 1], zdev[d])
+        gates, gate0, gate1 = select(mz, True)
+        own_gate[...] = jnp.where(mc == 0, gate0, gate1)
+        for e in range(EXPERTS):
+            gs[e, :, 0 : groups * ROWS] = lax.dot_general(
+                jnp.broadcast_to(gates[e], (8, 256)).astype(BF16), selz[mz, e], NT, preferred_element_type=F32
+            )
 
     def columns(k):
         return slice(k * width, (k + 1) * width)
 
     def start_raw(k):
         b = B_CHUNKS.index(k)
-        for d in (1, 3, 2):
+        swap_done(k)
+        for d in (1, 3):
             send(x2.at[:, columns(k)], raw_z.at[b, mz], zs.at[k, d - 1], zr.at[k, d - 1], zdev[d])
+
+    def relay_raw(k):
+        b = B_CHUNKS.index(k)
+        for d, part in ((1, pl.ds(0, 128)), (3, pl.ds(128, 128))):
+            z = lax.rem(mz - d + NZ, NZ)
+            arrived(raw_z.at[b, z], zr.at[k, d - 1])
+            ref = raw_z.at[b, z, part]
+            send(ref, ref, zs.at[k, 1 if d == 1 else 3], zr.at[k, 1 if d == 1 else 3], zdev[d])
 
     def pack(k):
         a = A_CHUNKS.index(k)
+        swap_done(k)
         for e in range(EXPERTS):
             block = jnp.dot(selz[mz, e], x2[:, columns(k)], preferred_element_type=F32)
             packed[a, e] = block.astype(BF16).reshape(groups, ROWS, width)
@@ -191,32 +238,44 @@
     def around_z(k):
         wait_x(k)
         ref = gt.at[mz] if k == NC else rows.at[k, mc, :, mz]
-        for d in (1, 3, 2):
+        for d in (1, 3, 2) if k == NC else (1, 3):
             send(ref, ref, zs.at[k, d - 1], zr.at[k, d - 1], zdev[d])
         if k < NC:
             send(ref, ref, bs.at[k, 0], br.at[k, 0], sibling)
 
     def cross_x(k):
         b = B_CHUNKS.index(k)
+        opposite = lax.rem(mz + 2, NZ)
+        arrived(raw_z.at[b, opposite, pl.ds(0, 128)], zr.at[k, 1])
+        arrived(raw_z.at[b, opposite, pl.ds(128, 128)], zr.at[k, 3])
         for d in range(NZ):
             z = lax.rem(mz + d, NZ)
-            if d:
-                arrived(raw_z.at[b, z], zr.at[k, NZ - d - 1])
             tokens = raw_z[b, z] if d else x2[:, columns(k)]
             for e in range(EXPERTS):
                 block = jnp.dot(selz[z, e], tokens, preferred_element_type=F32)
                 packed_z[b, e, :, z] = block.astype(BF16).reshape(groups, ROWS, width)
         start_x(k)
 
-    def take(k):
-        if k in A_CHUNKS:
-            for d in (1, 3, 2):
-                ref = rows.at[k, mc, :, lax.rem(mz - d + NZ, NZ)]
-                arrived(ref, zr.at[k, d - 1])
-                send(ref, ref, bs.at[k, d], br.at[k, d], sibling)
-        else:
-            wait_x(k)
-            send(rows.at[k, mc], rows.at[k, mc], bs.at[k, 0], br.at[k, 0], sibling)
+    def near(k):
+        for d, part in ((1, pl.ds(0, 2)), (3, pl.ds(2, 2))):
+            z = lax.rem(mz - d + NZ, NZ)
+            ref = rows.at[k, mc, :, z]
+            arrived(ref, zr.at[k, d - 1])
+            ref = rows.at[k, mc, :, z, part]
+            send(ref, ref, zs.at[k, 1 if d == 1 else 3], zr.at[k, 1 if d == 1 else 3], zdev[d])
+            ref = rows.at[k, mc, :, z]
+            send(ref, ref, bs.at[k, d], br.at[k, d], sibling)
+
+    def far(k):
+        opposite = lax.rem(mz + 2, NZ)
+        arrived(rows.at[k, mc, :, opposite, pl.ds(0, 2)], zr.at[k, 1])
+        arrived(rows.at[k, mc, :, opposite, pl.ds(2, 2)], zr.at[k, 3])
+        ref = rows.at[k, mc, :, opposite]
+        send(ref, ref, bs.at[k, 2], br.at[k, 2], sibling)
+
+    def whole(k):
+        wait_x(k)
+        send(rows.at[k, mc], rows.at[k, mc], bs.at[k, 0], br.at[k, 0], sibling)
 
     def shared(k):
         if k in A_CHUNKS:
@@ -250,23 +309,21 @@
             for copy in w_copies(i + 2):
                 copy.start()
 
-    start_x(NC)
-    for n, k in enumerate(A_CHUNKS):
-        pack(k)
-        if n:
-            start_x(A_CHUNKS[n - 1])
-        if n < len(B_CHUNKS):
-            start_raw(B_CHUNKS[n])
-    start_x(A_CHUNKS[-1])
+    def in_order(names):
+        steps = {
+            "t": start_raw, "r": relay_raw, "c": cross_x, "g": own_select, "p": pack, "x": start_x, "a": around_z,
+            "n": near, "f": far, "w": whole, "m": compute,
+        }
+        for word in names:
+            steps[word[0]](int(word[1:]))
+
+    in_order(FIRST)
     around_z(NC)
     for d in (1, 2, 3):
         z = lax.rem(mz + d, NZ)
         arrived(info.at[z], zr.at[NC + 1, NZ - d - 1])
         select(z)
-    for n, k in enumerate(A_CHUNKS):
-        around_z(k)
-        if n < len(B_CHUNKS):
-            cross_x(B_CHUNKS[n])
+    in_order(EARLY)
     perm = permutation(False)
 
     def place_saved(g, carry):
@@ -278,23 +335,39 @@
     lax.fori_loop(0, groups, place_saved, 0)
     for d in (1, 2, 3):
         arrived(gt.at[lax.rem(mz - d + NZ, NZ)], zr.at[NC, d - 1])
-    for i, ks in enumerate(ORDER):
-        for k in ks:
-            take(k)
-        if i:
-            compute(i - 1)
-    compute(len(ORDER) - 1)
+    in_order(LATE)
+    (k,) = ORDER[-1]
+    last = (len(ORDER) - 1) % 2
+    for copy in w_copies(len(ORDER) - 1):
+        copy.wait()
+
+    def term_of(at, h):
+        left = rows[k, h, at].reshape(big * 256, width)
+        term = lax.dot_general(left, wv[last, h], NT, preferred_element_type=F32)
+        return acc[at] + term.reshape(big, 256, term.shape[-1])
+
+    def own_half(m, carry):
+        at = pl.ds(m * big, big)
+        acc[at] = term_of(at, mc)
+        return carry
+
+    lax.fori_loop(0, 3, own_half, 0)
+    shared(k)
 
     lane = lax.broadcasted_iota(jnp.int32, (256, 256), 1)
     row16 = lax.broadcasted_iota(jnp.int32, (256, 256), 0) & 15
 
-    def dots(g, total):
-        raw = acc[g]
-        part = jnp.sum(raw * sv[g].astype(F32), axis=1, keepdims=True)
-        part = jnp.where(lane == row16 + g * 16, part, 0.0).reshape(16, 16, 256)
-        return total + jnp.sum(part, axis=1)
-
-    part = lax.fori_loop(0, groups, dots, jnp.zeros((16, 256), F32))
+    def dots(m, total):
+        at = pl.ds(m * big, big)
+        raw = term_of(at, 1 - mc)
+        acc[at] = raw
+        part = jnp.sum(raw * sv[at].astype(F32), axis=2, keepdims=True)
+        for n in range(big):
+            placed = jnp.where(lane == row16 + (m * big + n) * 16, part[n], 0.0)
+            total = total + jnp.sum(placed.reshape(16, 16, 256), axis=1)
+        return total
+
+    part = lax.fori_loop(0, 3, dots, jnp.zeros((16, 256), F32))
     pts[...] = jnp.broadcast_to(part[:, None, :], (16, 8, 256))
     slot = mx * NZ + mz
     own_part = pltpu.make_async_copy(pts.at[mz * NX + mx], pr.at[slot], loc_sem.at[NC + 1])
@@ -305,9 +378,12 @@
 
     gates = jnp.broadcast_to(gt[...].reshape(16, 8, 256)[:, 0:1, :], (16, 16, 256)).reshape(256, 256)
 
+    back = permutation(True)
+
     def finish(g, carry):
         gate = jnp.sum(jnp.where(lane == row16 + g * 16, gates, 0.0), axis=1, keepdims=True)
-        sv[g] = (gate * acc[g]).astype(BF16)
+        grad = (gate * acc[g]).astype(BF16)
+        sv[g] = jnp.dot(back, grad, preferred_element_type=F32).astype(BF16)
         pltpu.make_async_copy(sv.at[g], grad_hbm.at[g], o_sem.at[g]).start()
         return carry
 
@@ -343,7 +419,7 @@
         copy.wait_send()
 
 
-def expert_call(tokens, info, saved, weight, router):
+def expert_call(tokens, ids, logits, saved, weight, router):
     depth, hidden = tokens.shape[-1], weight.shape[0]
     groups = saved.shape[0]
     width = depth // 2 // NC
@@ -359,7 +435,7 @@
             jax.ShapeDtypeStruct(router.shape, F32),
             jax.ShapeDtypeStruct((8, 128), F32),
         ),
-        in_specs=[anywhere] * 5,
+        in_specs=[anywhere] * 6,
         out_specs=(anywhere, anywhere, anywhere, pl.BlockSpec(memory_space=pltpu.VMEM)),
         scratch_shapes=[
             pltpu.VMEM((NC, 2, groups, NZ, NX, ROWS, width), BF16),
@@ -367,7 +443,8 @@
             pltpu.VMEM((groups, 256, hidden), F32),
             pltpu.VMEM((groups, 256, hidden), BF16),
             pltpu.VMEM((256, depth // 2), BF16),
-            pltpu.VMEM((NZ, 2, 8, 128), F32),
+            pltpu.VMEM((NZ, 2) + ids.shape, jnp.int32),
+            pltpu.VMEM((2,) + ids.shape, F32),
             pltpu.VMEM((NZ, EXPERTS, groups * ROWS, 256), BF16),
             pltpu.VMEM((na, EXPERTS, groups, ROWS, width), BF16),
             pltpu.VMEM((nb, NZ, 256, width), BF16),
@@ -379,8 +456,8 @@
             pltpu.VMEM((16, 8, 256), F32),
             pltpu.VMEM((2, EXPERTS, 8, 256), F32),
             pltpu.VMEM((2, 8, 128), F32),
-            dma((2,)), dma((2, 4)), dma((groups,)), dma((groups,)), dma((NC + 2,)), dma((5,)), dma((5,)),
-            dma((NC + 1, 3)), dma((NC + 1, 3)), dma((NC + 2, 3)), dma((NC + 2, 3)), dma((NC + 1, 4)), dma((NC + 1, 4)),
+            dma((PIECES + 2,)), dma((2, 4)), dma((groups,)), dma((groups,)), dma((NC + 2,)), dma((5 + PIECES,)), dma((5 + PIECES,)),
+            dma((NC + 1, 3)), dma((NC + 1, 3)), dma((NC + 2, 4)), dma((NC + 2, 4)), dma((NC + 1, 4)), dma((NC + 1, 4)),
             dma((15,)), dma((15,)),
         ],
         compiler_params=pltpu.CompilerParams(
@@ -389,43 +466,64 @@
         cost_estimate=pl.CostEstimate(
             flops=2 * groups * 256 * depth * hidden, bytes_accessed=200_000_000, transcendentals=0
         ),
-    )(tokens, info, saved, weight, router)
-
-
-def last_kernel(grad_ref, tokens_ref, router_ref, spread_ref, hidden_ref, upstream_ref, perm):
-    @pl.when(pl.program_id(0) == 0)
-    def _():
-        perm[...] = permutation(True)
-
-    for g in range(grad_ref.shape[0]):
-        hidden_ref[g] = jnp.dot(perm[...], grad_ref[g], preferred_element_type=F32).astype(BF16)
+    )(tokens, ids, logits, saved, weight, router)
+
+
+def last_kernel(
+    grad_hbm, tokens_hbm, router_ref, spread_ref, hidden_hbm, upstream_hbm,
+    grad, tokens, upstream, grad_in, grad_out, token_in, token_out,
+):
+    groups, pieces = grad.shape[0], tokens.shape[0]
+    width = tokens.shape[2]
+    reads, token_reads, writes = [], [], []
+    for q in range(pieces):
+        cols = pl.ds(q * width, width)
+        token_reads.append(pltpu.make_async_copy(tokens_hbm.at[:, cols], tokens.at[q], token_in.at[q]))
+        token_reads[q].start()
+    for g in range(groups):
+        reads.append(pltpu.make_async_copy(grad_hbm.at[g], grad.at[g], grad_in.at[g]))
+        reads[g].start()
+
+    def write(src, dst, sem):
+        writes.append(pltpu.make_async_copy(src, dst, sem))
+        writes[-1].start()
+
     live = lax.axis_index("section") < lax.axis_size("section") - 1
     spread = jnp.transpose(spread_ref[...])
-    total = tokens_ref[...].astype(F32)
-    for e in range(EXPERTS):
-        total = total + spread[:, e : e + 1] * router_ref[e : e + 1, :]
-    upstream_ref[...] = jnp.where(live, total, 0.0).astype(BF16)
+    for q in range(pieces):
+        token_reads[q].wait()
+        total = tokens[q].astype(F32)
+        for e in range(EXPERTS):
+            total = total + spread[:, e : e + 1] * router_ref[e : e + 1, q * width : (q + 1) * width]
+        upstream[q] = jnp.where(live, total, 0.0).astype(BF16)
+        write(upstream.at[q], upstream_hbm.at[:, pl.ds(q * width, width)], token_out.at[q])
+        for g in range(q * groups // pieces, (q + 1) * groups // pieces):
+            reads[g].wait()
+            write(grad.at[g], hidden_hbm.at[g], grad_out.at[g])
+    for copy in writes:
+        copy.wait()
 
 
 def last_call(grad, tokens, router, spread):
-    groups, rows, hidden = grad.shape
+    groups = grad.shape[0]
     flat, depth = tokens.shape
-    steps = 3
-    grad_spec = pl.BlockSpec((groups // steps, rows, hidden), lambda s: (s, 0, 0))
-    token_spec = pl.BlockSpec((flat, depth // steps), lambda s: (0, s))
+    pieces = 4
+    anywhere = pl.BlockSpec(memory_space=pl.ANY)
+    whole = pl.BlockSpec(memory_space=pltpu.VMEM)
+    dma = pltpu.SemaphoreType.DMA
     return pl.pallas_call(
         last_kernel,
         name="last",
-        grid=(steps,),
         out_shape=(jax.ShapeDtypeStruct(grad.shape, BF16), jax.ShapeDtypeStruct(tokens.shape, BF16)),
-        in_specs=[
-            grad_spec,
-            token_spec,
-            pl.BlockSpec((EXPERTS, depth // steps), lambda s: (0, s)),
-            pl.BlockSpec((8, 128), lambda s: (0, 0)),
+        in_specs=[anywhere, anywhere, whole, whole],
+        out_specs=(anywhere, anywhere),
+        scratch_shapes=[
+            pltpu.VMEM(grad.shape, BF16),
+            pltpu.VMEM((pieces, flat, depth // pieces), BF16),
+            pltpu.VMEM((pieces, flat, depth // pieces), BF16),
+            dma((groups,)), dma((groups,)), dma((pieces,)), dma((pieces,)),
         ],
-        out_specs=(grad_spec, token_spec),
-        scratch_shapes=[pltpu.VMEM((256, 256), BF16)],
+        compiler_params=pltpu.CompilerParams(vmem_limit_bytes=67043328),
     )(grad, tokens, router, spread)
 
 
@@ -433,16 +531,9 @@
     micro, per, depth = upstream_dy.shape[1:]
     hidden = down_weight.shape[1]
     flat = micro * per
-    info = jnp.concatenate(
-        [
-            expert_ids[0].transpose(2, 0, 1).reshape(2, flat).astype(F32),
-            gate_logits[0].transpose(2, 0, 1).reshape(2, flat),
-            jnp.zeros((4, flat), F32),
-        ]
-    )
     saved = saved_hidden[0].transpose(0, 2, 1, 3).reshape(micro * CAP // 8, 256, hidden)
     grad, tokens, router, spread = expert_call(
-        upstream_dy[0].reshape(flat, depth), info, saved, down_weight[0], router_weight[0].T
+        upstream_dy[0].reshape(flat, depth), expert_ids[0].transpose(0, 2, 1), gate_logits[0].transpose(0, 2, 1), saved, down_weight[0], router_weight[0].T
     )
     hidden_grad, upstream = last_call(grad, tokens, router, spread)
     hidden_grad = hidden_grad.reshape(micro, CAP, NX * NZ * 2, hidden).transpose(0, 2, 1, 3)

time: 163 us -> 130 us (0.80)
  Pallas kernels: 160 us -> 129 us
    pallas_call x1, Pallas kernels: 152 us -> 123 us  [expert_call(): pl.pallas_call(functools.partial(expert_kernel, groups, width), name='exp...]
    pallas_call x1, Pallas kernels: 7.67 us -> 5.91 us  [last_call(): pl.pallas_call(last_kernel, name='last', out_shape=(jax.ShapeDtypeStruct(...]
where the time goes in v3:
time: 130 us
  Pallas kernels  129 us (99%)
    pallas_call x1, Pallas kernels, expert_call(): pl.pallas_call(functools.partial(expert_kernel, groups, width), name='exp...  123 us
    pallas_call x1, Pallas kernels, last_call(): pl.pallas_call(last_kernel, name='last', out_shape=(jax.ShapeDtypeStruct(...  5.91 us

profile of v3, /device:TPU:1, one launch (start us, length us, event | category | flops | bytes accessed | tf_op | source)
XLA Modules:
  0.0 129.5 jit_solution(10338597094415731294)
XLA Ops:
  0.6 122.8 %experts.1 = (bf16[9,256,1024]{2,1,0:T(8,128)(2,1)}, bf16[128,6144]{1,0:T(8,128)(2,1)}, f32[4,6144]{1,0:T(4,128)}, f32[8,128]{1,0:T(8,128)}) custom-call(bf16[128,6144]{1,0:T(8,128)(2,1)} %bitcast.25, s32[2,2,64]{2,1,0:T(2,128)} %bitcast.28, f32[2,2,64]{2,1,0:T(2,128)} %bitcast.29, bf16[9,256,1024]{2,1,0:T(8,128)(2,1)} %bitcast.23, ...), custom_call_target="tpu_custom_call" | custom-call | flops 28991029248 | bytes 200000000 | tf_op jit(solution)/shard_map/experts/pallas_call | solution.py:429
  123.5 5.9 %last.1 = (bf16[9,256,1024]{2,1,0:T(8,128)(2,1)}, bf16[128,6144]{1,0:T(8,128)(2,1)}) custom-call(bf16[9,256,1024]{2,1,0:T(8,128)(2,1)} %get-tuple-element.8.grad_hbm, bf16[128,6144]{1,0:T(8,128)(2,1)} %get-tuple-element.9.tokens_hbm, f32[4,6144]{1,0:T(4,128)} %get-tuple-element.10.router_ref, f32[8,128]{1,0:T(8,128)} %get-tuple-element.11.spread_ref), custom_call_target="tpu_custom_call" | custom-call | tf_op jit(solution)/shard_map/last/pallas_call | solution.py:514

commit v4 on v3

--- a/solution.py
+++ b/solution.py
@@ -14,8 +14,11 @@
 NC = 12
 A_CHUNKS = (0, 2, 4, 6, 8, 10, 11)
 B_CHUNKS = (1, 3, 5, 7, 9)
-ORDER = ((1, 0), (3, 2), (4, 5), (6, 7), (8,), (10,), (9,), (11,))
-PIECES = 12
+PASSES = ((1, 0), (3, 2), (4, 5), (6,), (7,), (8,), (10,))
+ORDER = (1, 0, 3, 2, 4, 5, 6, 7, 8, 10, 9, 11)
+THIRDS = 9
+HELD = 6
+PIECES = 4
 FIRST = (
     "t1", "g12", "x12", "p0", "p2", "x0", "t3", "t5", "p4", "x2", "t7", "p6",
     "x4", "p8", "x6", "t9", "p10", "x8", "p11", "x10", "x11",
@@ -24,9 +27,11 @@
     "r1", "r3", "a0", "r5", "c1", "r7", "c3", "r9", "a2", "c5", "c7", "c9",
 )
 LATE = (
-    "n0", "a4", "n2", "a6", "w1", "f0", "m0", "n4", "a8", "w3", "f2", "m1",
-    "n6", "a10", "f4", "w5", "n8", "a11", "m2", "f6", "n10", "w7", "m3", "f8",
-    "n11", "m4", "f10", "w9", "m5", "f11", "m6",
+    "n0", "s0", "a4", "w101", "w201", "n2", "a6", "w301", "s2", "f0", "m0", "n4",
+    "a8", "w103", "w203", "s4", "w303", "f2", "m1", "n6", "a10", "w105", "w205", "f4",
+    "s6", "w305", "n8", "m2", "w107", "f6", "s8", "w207", "m3", "n10", "a11", "w307",
+    "s10", "m4", "f8", "f10", "w109", "m5", "w209", "m109", "n11", "s11", "m6", "w309",
+    "m209", "f11", "m309",
 )
 ROWS = 16
 MESH = pl.DeviceIdType.MESH
@@ -66,8 +71,8 @@
 
 def expert_kernel(
     groups, width, x_hbm, ids_hbm, logits_hbm, saved_hbm, w_hbm, router_hbm, grad_hbm, next_hbm, nrouter_hbm, spread_ref,
-    rows, wv, acc, sv, x2, info, logits, selz, packed, raw_z, packed_z, gs, gt, own_gate, pts, pr, sums, spread,
-    x_sem, w_sem, s_sem, o_sem, loc_sem, b0_send, b0_recv, xs, xr, zs, zr, bs, br, ps, pr_sem,
+    rows, wv, acc, sv, x2, info, logits, selz, packed, raw_z, packed_z, gs, gt, next_gate, next_sel, next_ids, next_logits, pts, pr, sums, next_sums,
+    x_sem, w_sem, s_sem, o_sem, loc_sem, sent, b0_recv, xa, xb, zr, br, pr_sem, next_sem,
 ):
     me = lax.axis_index("expert")
     section = lax.axis_index("section")
@@ -82,6 +87,7 @@
     xdev = [dev(mx + d, mz, mc) for d in range(NX)]
     zdev = [dev(mx, mz + d, mc) for d in range(NZ)]
     before, after = dev(mx, mz, mc, -1), dev(mx, mz, mc, 1)
+    before_other, after_other = dev(mx, mz, 1 - mc, -1), dev(mx, mz, 1 - mc, 1)
     chips = [(dx, dz) for dx in range(NX) for dz in range(NZ) if dx or dz]
 
     def remote(src, dst, send, recv, target):
@@ -89,15 +95,14 @@
             src_ref=src, dst_ref=dst, send_sem=send, recv_sem=recv, device_id=target, device_id_type=MESH
         )
 
-    waits = []
-
-    def send(src, dst, send_sem, recv_sem, target):
-        copy = remote(src, dst, send_sem, recv_sem, target)
-        copy.start()
-        waits.append(copy)
+    def send(src, dst, recv_sem, target, kind):
+        remote(src, dst, sent.at[kind], recv_sem, target).start()
+
+    def drain(ref, kind):
+        remote(ref, ref, sent.at[kind], b0_recv.at[0], sibling).wait_send()
 
     def arrived(ref, sem):
-        remote(ref, ref, b0_send.at[0], sem, sibling).wait_recv()
+        remote(ref, ref, sent.at[0], sem, sibling).wait_recv()
 
     mine_rows = pl.ds(pl.multiple_of(mc * 128, 128), 128)
     sib_rows = pl.ds(pl.multiple_of((1 - mc) * 128, 128), 128)
@@ -115,17 +120,17 @@
         own_x[q].start()
 
     barrier = pltpu.get_barrier_semaphore()
-    partners = [sibling, before, after] + [dev(mx + dx, mz + dz, mc) for dx, dz in chips]
+    partners = [sibling, before, after, before_other, after_other] + [dev(mx + dx, mz + dz, mc) for dx, dz in chips]
     for target in partners:
         pl.semaphore_signal(barrier, inc=1, device_id=target, device_id_type=MESH)
     pl.semaphore_wait(barrier, len(partners))
 
-    send(ids_hbm, info.at[mz, mc], b0_send.at[1], b0_recv.at[1], sibling)
-    send(logits_hbm, logits.at[mc], b0_send.at[0], b0_recv.at[0], sibling)
+    send(ids_hbm, info.at[mz, mc], b0_recv.at[1], sibling, 10)
+    send(logits_hbm, logits.at[mc], b0_recv.at[0], sibling, 11)
     for q in range(PIECES):
         cols = pl.ds(pl.multiple_of((1 - mc) * half + q * piece, 128), piece)
         to = x2.at[mine_rows, q * piece : (q + 1) * piece]
-        send(x_hbm.at[:, cols], to, b0_send.at[5 + q], b0_recv.at[5 + q], sibling)
+        send(x_hbm.at[:, cols], to, b0_recv.at[6 + q], sibling, 8)
     swapped = set()
 
     def swap_done(k):
@@ -133,26 +138,25 @@
         if q not in swapped:
             swapped.add(q)
             own_x[q].wait()
-            arrived(x2.at[sib_rows, q * piece : (q + 1) * piece], b0_recv.at[5 + q])
-
-    def w_copies(i):
+            arrived(x2.at[sib_rows, q * piece : (q + 1) * piece], b0_recv.at[6 + q])
+
+    def w_copies(k):
+        slot = ORDER.index(k) % HELD
         copies = []
-        for n, k in enumerate(ORDER[i]):
-            for h in range(2):
-                cols = pl.ds(h * half + k * width, width)
-                copies.append(
-                    pltpu.make_async_copy(w_hbm.at[:, cols], wv.at[i % 2, n * 2 + h], w_sem.at[i % 2, n * 2 + h])
-                )
+        for h in range(2):
+            cols = pl.ds(h * half + k * width, width)
+            copies.append(pltpu.make_async_copy(w_hbm.at[:, cols], wv.at[slot, h], w_sem.at[slot]))
         return copies
 
-    for i in range(2):
-        for copy in w_copies(i):
+    for k in ORDER[:HELD]:
+        for copy in w_copies(k):
             copy.start()
-    s_copy = [pltpu.make_async_copy(saved_hbm.at[g], sv.at[g], s_sem.at[g]) for g in range(groups)]
-    for copy in s_copy:
-        copy.start()
-    send(x_hbm, next_hbm, b0_send.at[2], b0_recv.at[2], before)
-    send(router_hbm, nrouter_hbm, b0_send.at[3], b0_recv.at[3], before)
+    s_copy = [pltpu.make_async_copy(saved_hbm, sv, s_sem.at[0])]
+    s_copy[0].start()
+    send(ids_hbm, next_ids, b0_recv.at[4], before, 15)
+    send(logits_hbm, next_logits, b0_recv.at[5], before, 14)
+    send(x_hbm, next_hbm, b0_recv.at[2], before, 12)
+    send(router_hbm, nrouter_hbm, b0_recv.at[3], before, 13)
 
     def select(z, own=False):
         code0, gate0 = codes_of(info[z, 0], logits[0] if own else None, 0)
@@ -164,7 +168,7 @@
             selz[z, e] = (row == code).astype(F32).astype(BF16)
             if own:
                 gates.append(jnp.concatenate([gate0[e : e + 1], gate1[e : e + 1]], axis=1))
-        return gates, gate0, gate1
+        return gates
 
     gs[...] = jnp.zeros_like(gs)
 
@@ -174,9 +178,8 @@
         arrived(info.at[mz, 1 - mc], b0_recv.at[1])
         arrived(logits.at[1 - mc], b0_recv.at[0])
         for d in (1, 3, 2):
-            send(info.at[mz], info.at[mz], zs.at[NC + 1, d - 1], zr.at[NC + 1, d - 1], zdev[d])
-        gates, gate0, gate1 = select(mz, True)
-        own_gate[...] = jnp.where(mc == 0, gate0, gate1)
+            send(info.at[mz], info.at[mz], zr.at[NC + 1, d - 1], zdev[d], 5)
+        gates = select(mz, True)
         for e in range(EXPERTS):
             gs[e, :, 0 : groups * ROWS] = lax.dot_general(
                 jnp.broadcast_to(gates[e], (8, 256)).astype(BF16), selz[mz, e], NT, preferred_element_type=F32
@@ -185,11 +188,15 @@
     def columns(k):
         return slice(k * width, (k + 1) * width)
 
+    third = groups // 3
+
+    parts = [pl.ds(p * third, third) for p in range(3)]
+
     def start_raw(k):
         b = B_CHUNKS.index(k)
         swap_done(k)
         for d in (1, 3):
-            send(x2.at[:, columns(k)], raw_z.at[b, mz], zs.at[k, d - 1], zr.at[k, d - 1], zdev[d])
+            send(x2.at[:, columns(k)], raw_z.at[b, mz], zr.at[k, d - 1], zdev[d], 3)
 
     def relay_raw(k):
         b = B_CHUNKS.index(k)
@@ -197,7 +204,7 @@
             z = lax.rem(mz - d + NZ, NZ)
             arrived(raw_z.at[b, z], zr.at[k, d - 1])
             ref = raw_z.at[b, z, part]
-            send(ref, ref, zs.at[k, 1 if d == 1 else 3], zr.at[k, 1 if d == 1 else 3], zdev[d])
+            send(ref, ref, zr.at[k, 1], zdev[d], 3)
 
     def pack(k):
         a = A_CHUNKS.index(k)
@@ -210,44 +217,47 @@
 
     def start_x(k):
         if k == NC:
-            here = gs.at
-            there = gt.at[mz, mx]
+            locals_[k] = pltpu.make_async_copy(gs.at[mx], gt.at[mz, mx], loc_sem.at[k])
         elif k in A_CHUNKS:
-            here = packed.at[A_CHUNKS.index(k)].at
-            there = rows.at[k, mc, :, mz, mx]
+            locals_[k] = pltpu.make_async_copy(
+                packed.at[A_CHUNKS.index(k), mx], rows.at[k, mc, :, mz, mx], loc_sem.at[k]
+            )
         else:
-            here = packed_z.at[B_CHUNKS.index(k)].at
-            there = rows.at[k, mc, :, :, mx]
-        locals_[k] = pltpu.make_async_copy(here[mx], there, loc_sem.at[k])
+            locals_[k] = pltpu.make_async_copy(
+                packed_z.at[B_CHUNKS.index(k), mx], rows.at[k, mc, :, :, mx], loc_sem.at[k]
+            )
         locals_[k].start()
-        for d in (2, 1, 3):
-            send(here[lax.rem(mx + d, NX)], there, xs.at[k, d - 1], xr.at[k, d - 1], xdev[d])
-
-    def wait_x(k):
+        for p, at in enumerate(parts if k in B_CHUNKS else parts[:1]):
+            for d in (2, 1, 3):
+                e = lax.rem(mx + d, NX)
+                if k == NC:
+                    send(gs.at[e], gt.at[mz, mx], xa.at[len(A_CHUNKS), d - 1], xdev[d], 6)
+                elif k in A_CHUNKS:
+                    a = A_CHUNKS.index(k)
+                    send(packed.at[a, e], rows.at[k, mc, :, mz, mx], xa.at[a, d - 1], xdev[d], 0)
+                else:
+                    b = B_CHUNKS.index(k)
+                    send(packed_z.at[b, e, at], rows.at[k, mc, at, :, mx], xb.at[b, d - 1, p], xdev[d], 1)
+
+    def around_z(k):
         locals_[k].wait()
         for d in (1, 2, 3):
             x = lax.rem(mx - d + NX, NX)
-            if k == NC:
-                ref = gt.at[mz, x]
-            elif k in A_CHUNKS:
-                ref = rows.at[k, mc, :, mz, x]
-            else:
-                ref = rows.at[k, mc, :, :, x]
-            arrived(ref, xr.at[k, d - 1])
-
-    def around_z(k):
-        wait_x(k)
-        ref = gt.at[mz] if k == NC else rows.at[k, mc, :, mz]
-        for d in (1, 3, 2) if k == NC else (1, 3):
-            send(ref, ref, zs.at[k, d - 1], zr.at[k, d - 1], zdev[d])
-        if k < NC:
-            send(ref, ref, bs.at[k, 0], br.at[k, 0], sibling)
+            a = len(A_CHUNKS) if k == NC else A_CHUNKS.index(k)
+            arrived(gt.at[mz, x] if k == NC else rows.at[k, mc, :, mz, x], xa.at[a, d - 1])
+        if k == NC:
+            for d in (1, 3, 2):
+                send(gt.at[mz], gt.at[mz], zr.at[k, d - 1], zdev[d], 7)
+            return
+        ref = rows.at[k, mc, :, mz]
+        for d in (1, 3):
+            send(ref, ref, zr.at[k, d - 1], zdev[d], 2)
+        send(ref, ref, br.at[k, 0], sibling, 4)
 
     def cross_x(k):
         b = B_CHUNKS.index(k)
         opposite = lax.rem(mz + 2, NZ)
-        arrived(raw_z.at[b, opposite, pl.ds(0, 128)], zr.at[k, 1])
-        arrived(raw_z.at[b, opposite, pl.ds(128, 128)], zr.at[k, 3])
+        arrived(raw_z.at[b, opposite], zr.at[k, 1])
         for d in range(NZ):
             z = lax.rem(mz + d, NZ)
             tokens = raw_z[b, z] if d else x2[:, columns(k)]
@@ -257,62 +267,78 @@
         start_x(k)
 
     def near(k):
-        for d, part in ((1, pl.ds(0, 2)), (3, pl.ds(2, 2))):
+        for d, share in ((1, pl.ds(0, 2)), (3, pl.ds(2, 2))):
             z = lax.rem(mz - d + NZ, NZ)
-            ref = rows.at[k, mc, :, z]
-            arrived(ref, zr.at[k, d - 1])
-            ref = rows.at[k, mc, :, z, part]
-            send(ref, ref, zs.at[k, 1 if d == 1 else 3], zr.at[k, 1 if d == 1 else 3], zdev[d])
-            ref = rows.at[k, mc, :, z]
-            send(ref, ref, bs.at[k, d], br.at[k, d], sibling)
+            arrived(rows.at[k, mc, :, z], zr.at[k, d - 1])
+            ref = rows.at[k, mc, :, z, share]
+            send(ref, ref, zr.at[k, 1], zdev[d], 2)
+
+    def near_shared(k):
+        for d in (1, 3):
+            ref = rows.at[k, mc, :, lax.rem(mz - d + NZ, NZ)]
+            send(ref, ref, br.at[k, 0], sibling, 4)
 
     def far(k):
-        opposite = lax.rem(mz + 2, NZ)
-        arrived(rows.at[k, mc, :, opposite, pl.ds(0, 2)], zr.at[k, 1])
-        arrived(rows.at[k, mc, :, opposite, pl.ds(2, 2)], zr.at[k, 3])
-        ref = rows.at[k, mc, :, opposite]
-        send(ref, ref, bs.at[k, 2], br.at[k, 2], sibling)
-
-    def whole(k):
-        wait_x(k)
-        send(rows.at[k, mc], rows.at[k, mc], bs.at[k, 0], br.at[k, 0], sibling)
+        ref = rows.at[k, mc, :, lax.rem(mz + 2, NZ)]
+        arrived(ref, zr.at[k, 1])
+        send(ref, ref, br.at[k, 0], sibling, 4)
+
+    def whole(step):
+        k, p = step % 100, step // 100 - 1
+        b, at = B_CHUNKS.index(k), parts[p]
+        if p == 0:
+            locals_[k].wait()
+        for d in (1, 2, 3):
+            arrived(rows.at[k, mc, at, :, lax.rem(mx - d + NX, NX)], xb.at[b, d - 1, p])
+        send(rows.at[k, mc, at], rows.at[k, mc, at], br.at[k, p if k == THIRDS else 0], sibling, 4)
 
     def shared(k):
-        if k in A_CHUNKS:
-            for d in range(NZ):
-                arrived(rows.at[k, 1 - mc, :, lax.rem(mz - d + NZ, NZ)], br.at[k, d])
-        else:
-            arrived(rows.at[k, 1 - mc], br.at[k, 0])
-
-    big = groups // 3
-
-    def compute(i):
-        for k in ORDER[i]:
+        arrived(rows.at[k, 1 - mc], br.at[k, 0])
+
+    def terms(ks, at):
+        total = None
+        for k in ks:
+            slot = ORDER.index(k) % HELD
+            for h in range(2):
+                left = rows[k, h, at].reshape(third * 256, width)
+                term = lax.dot_general(left, wv[slot, h], NT, preferred_element_type=F32)
+                total = term if total is None else total + term
+        return total.reshape(third, 256, total.shape[-1])
+
+    def w_ready(k):
+        slot = ORDER.index(k) % HELD
+        pltpu.make_async_copy(wv.at[slot], wv.at[slot], w_sem.at[slot]).wait()
+
+    def compute(step):
+        if step >= 100:
+            k, p = step % 100, step // 100 - 1
+            arrived(rows.at[k, 1 - mc, parts[p]], br.at[k, p])
+            if p == 0:
+                w_ready(k)
+            acc[parts[p]] += terms((k,), parts[p])
+            return
+        ks = PASSES[step]
+        for k in ks:
             shared(k)
-        for copy in w_copies(i):
-            copy.wait()
+            w_ready(k)
 
         def body(m, carry):
-            at = pl.ds(m * big, big)
-            total = None
-            for n, k in enumerate(ORDER[i]):
-                for h in range(2):
-                    left = rows[k, h, at].reshape(big * 256, width)
-                    term = lax.dot_general(left, wv[i % 2, n * 2 + h], NT, preferred_element_type=F32)
-                    total = term if total is None else total + term
-            total = total.reshape(big, 256, total.shape[-1])
-            acc[at] = total if i == 0 else acc[at] + total
+            at = pl.ds(m * third, third)
+            total = terms(ks, at)
+            acc[at] = total if step == 0 else acc[at] + total
             return carry
 
         lax.fori_loop(0, 3, body, 0)
-        if i + 2 < len(ORDER):
-            for copy in w_copies(i + 2):
-                copy.start()
+        for k in ks:
+            later = ORDER.index(k) + HELD
+            if later < len(ORDER):
+                for copy in w_copies(ORDER[later]):
+                    copy.start()
 
     def in_order(names):
         steps = {
             "t": start_raw, "r": relay_raw, "c": cross_x, "g": own_select, "p": pack, "x": start_x, "a": around_z,
-            "n": near, "f": far, "w": whole, "m": compute,
+            "n": near, "f": far, "w": whole, "m": compute, "s": near_shared,
         }
         for word in names:
             steps[word[0]](int(word[1:]))
@@ -330,40 +356,32 @@
         sv[g] = jnp.dot(perm, sv[g], preferred_element_type=F32).astype(BF16)
         return carry
 
+    arrived(next_ids, b0_recv.at[4])
+    arrived(next_logits, b0_recv.at[5])
+    code, gate = codes_of(next_ids, next_logits, mc.astype(F32))
+    next_gate[...] = gate
+    row = lax.broadcasted_iota(jnp.int32, (groups * ROWS, 128), 0).astype(F32)
+    for e in range(EXPERTS):
+        next_sel[e] = (row == code[e : e + 1]).astype(F32)
     for copy in s_copy:
         copy.wait()
     lax.fori_loop(0, groups, place_saved, 0)
     for d in (1, 2, 3):
         arrived(gt.at[lax.rem(mz - d + NZ, NZ)], zr.at[NC, d - 1])
     in_order(LATE)
-    (k,) = ORDER[-1]
-    last = (len(ORDER) - 1) % 2
-    for copy in w_copies(len(ORDER) - 1):
-        copy.wait()
-
-    def term_of(at, h):
-        left = rows[k, h, at].reshape(big * 256, width)
-        term = lax.dot_general(left, wv[last, h], NT, preferred_element_type=F32)
-        return acc[at] + term.reshape(big, 256, term.shape[-1])
-
-    def own_half(m, carry):
-        at = pl.ds(m * big, big)
-        acc[at] = term_of(at, mc)
-        return carry
-
-    lax.fori_loop(0, 3, own_half, 0)
-    shared(k)
-
     lane = lax.broadcasted_iota(jnp.int32, (256, 256), 1)
     row16 = lax.broadcasted_iota(jnp.int32, (256, 256), 0) & 15
 
+    shared(ORDER[-1])
+    w_ready(ORDER[-1])
+
     def dots(m, total):
-        at = pl.ds(m * big, big)
-        raw = term_of(at, 1 - mc)
+        at = pl.ds(m * third, third)
+        raw = acc[at] + terms(ORDER[-1:], at)
         acc[at] = raw
         part = jnp.sum(raw * sv[at].astype(F32), axis=2, keepdims=True)
-        for n in range(big):
-            placed = jnp.where(lane == row16 + (m * big + n) * 16, part[n], 0.0)
+        for n in range(third):
+            placed = jnp.where(lane == row16 + (m * third + n) * 16, part[n], 0.0)
             total = total + jnp.sum(placed.reshape(16, 16, 256), axis=1)
         return total
 
@@ -374,7 +392,7 @@
     own_part.start()
     for n, (dx, dz) in enumerate(chips):
         x, z = lax.rem(mx + dx, NX), lax.rem(mz + dz, NZ)
-        send(pts.at[z * NX + x], pr.at[slot], ps.at[n], pr_sem.at[n], dev(x, z, mc))
+        send(pts.at[z * NX + x], pr.at[slot], pr_sem.at[n], dev(x, z, mc), 9)
 
     gates = jnp.broadcast_to(gt[...].reshape(16, 8, 256)[:, 0:1, :], (16, 16, 256)).reshape(256, 256)
 
@@ -384,7 +402,7 @@
         gate = jnp.sum(jnp.where(lane == row16 + g * 16, gates, 0.0), axis=1, keepdims=True)
         grad = (gate * acc[g]).astype(BF16)
         sv[g] = jnp.dot(back, grad, preferred_element_type=F32).astype(BF16)
-        pltpu.make_async_copy(sv.at[g], grad_hbm.at[g], o_sem.at[g]).start()
+        pltpu.make_async_copy(sv.at[g], grad_hbm.at[g], o_sem.at[0]).start()
         return carry
 
     lax.fori_loop(0, groups, finish, 0)
@@ -394,29 +412,33 @@
         x, z = lax.rem(mx - dx + NX, NX), lax.rem(mz - dz + NZ, NZ)
         arrived(pr.at[x * NZ + z], pr_sem.at[n])
     summed = jnp.sum(pr[...].reshape(EXPERTS, NZ, 8, 256), axis=1)
-    sums[0] = summed
-    send(sums.at[0], sums.at[1], bs.at[NC, 0], br.at[NC, 0], sibling)
-    arrived(sums.at[1], br.at[NC, 0])
-    summed = summed + sums[1]
-    token = []
-    for e in range(EXPERTS):
-        chosen = jnp.where(mc == 0, selz[mz, e, :, 0:128].astype(F32), selz[mz, e, :, 128:256].astype(F32))
-        token.append(
-            jnp.dot(summed[e, :, 0 : groups * ROWS], chosen, preferred_element_type=F32, precision=HIGHEST)[0:1]
-        )
-    token = jnp.concatenate(token * 2, axis=0)
-    gate = own_gate[...]
-    mixed = jnp.sum((gate * token)[0:EXPERTS], axis=0, keepdims=True)
-    spread[0] = gate * (token - mixed)
-    send(spread.at[0], spread.at[1], b0_send.at[4], b0_recv.at[4], before)
-    for g in range(groups):
-        pltpu.make_async_copy(sv.at[g], grad_hbm.at[g], o_sem.at[g]).wait()
+    sums[...] = summed
+    send(sums, next_sums.at[mc], next_sem.at[mc], before, 16)
+    send(sums, next_sums.at[mc], next_sem.at[mc], before_other, 16)
+    pltpu.make_async_copy(sv, grad_hbm, o_sem.at[0]).wait()
     arrived(next_hbm, b0_recv.at[2])
     arrived(nrouter_hbm, b0_recv.at[3])
-    arrived(spread.at[1], b0_recv.at[4])
-    spread_ref[...] = spread[1]
-    for copy in waits:
-        copy.wait_send()
+    arrived(next_sums.at[0], next_sem.at[0])
+    arrived(next_sums.at[1], next_sem.at[1])
+    total = next_sums[0] + next_sums[1]
+    token = [
+        jnp.dot(total[e, :, 0 : groups * ROWS], next_sel[e], preferred_element_type=F32, precision=HIGHEST)[0:1]
+        for e in range(EXPERTS)
+    ]
+    token = jnp.concatenate(token * 2, axis=0)
+    gate = next_gate[...]
+    mixed = jnp.sum((gate * token)[0:EXPERTS], axis=0, keepdims=True)
+    spread_ref[...] = gate * (token - mixed)
+    three = pl.ds(0, 3)
+    na = len(A_CHUNKS)
+    for kind, ref in enumerate(
+        (
+            packed.at[:, three], packed_z.at[:, three], rows.at[pl.ds(0, na), 0, :, three], raw_z.at[:, three],
+            rows.at[:, 0], info.at[three], gs.at[three], gt.at[three], x2.at[pl.ds(0, 128), :], pts.at[pl.ds(0, 15)],
+            info.at[0, 0], logits.at[0], next_hbm, nrouter_hbm, next_logits, next_ids, next_sums,
+        )
+    ):
+        drain(ref, kind)
 
 
 def expert_call(tokens, ids, logits, saved, weight, router):
@@ -439,7 +461,7 @@
         out_specs=(anywhere, anywhere, anywhere, pl.BlockSpec(memory_space=pltpu.VMEM)),
         scratch_shapes=[
             pltpu.VMEM((NC, 2, groups, NZ, NX, ROWS, width), BF16),
-            pltpu.VMEM((2, 4, hidden, width), BF16),
+            pltpu.VMEM((HELD, 2, hidden, width), BF16),
             pltpu.VMEM((groups, 256, hidden), F32),
             pltpu.VMEM((groups, 256, hidden), BF16),
             pltpu.VMEM((256, depth // 2), BF16),
@@ -452,13 +474,15 @@
             pltpu.VMEM((EXPERTS, 8, 256), F32),
             pltpu.VMEM((NZ, NX, 8, 256), F32),
             pltpu.VMEM((8, 128), F32),
+            pltpu.VMEM((EXPERTS, groups * ROWS, 128), F32),
+            pltpu.VMEM(ids.shape, jnp.int32),
+            pltpu.VMEM(ids.shape, F32),
             pltpu.VMEM((16, 8, 256), F32),
             pltpu.VMEM((16, 8, 256), F32),
+            pltpu.VMEM((EXPERTS, 8, 256), F32),
             pltpu.VMEM((2, EXPERTS, 8, 256), F32),
-            pltpu.VMEM((2, 8, 128), F32),
-            dma((PIECES + 2,)), dma((2, 4)), dma((groups,)), dma((groups,)), dma((NC + 2,)), dma((5 + PIECES,)), dma((5 + PIECES,)),
-            dma((NC + 1, 3)), dma((NC + 1, 3)), dma((NC + 2, 4)), dma((NC + 2, 4)), dma((NC + 1, 4)), dma((NC + 1, 4)),
-            dma((15,)), dma((15,)),
+            dma((PIECES + 2,)), dma((HELD,)), dma((1,)), dma((1,)), dma((NC + 2,)), dma((17,)), dma((6 + PIECES,)),
+            dma((na + 1, 3)), dma((nb, 3, 3)), dma((NC + 2, 3)), dma((NC, 3)), dma((15,)), dma((2,)),
         ],
         compiler_params=pltpu.CompilerParams(
             collective_id=0, has_side_effects=True, vmem_limit_bytes=67043328

time: 130 us -> 127 us (0.977)
  Pallas kernels: 129 us -> 126 us
    pallas_call x1, Pallas kernels: 123 us -> 120 us  [expert_call(): pl.pallas_call(functools.partial(expert_kernel, groups, width), name='exp...]
where the time goes in v4:
time: 127 us
  Pallas kernels  126 us (99%)
    pallas_call x1, Pallas kernels, expert_call(): pl.pallas_call(functools.partial(expert_kernel, groups, width), name='exp...  120 us
    pallas_call x1, Pallas kernels, last_call(): pl.pallas_call(last_kernel, name='last', out_shape=(jax.ShapeDtypeStruct(...  5.91 us

profile of v4, /device:TPU:1, one launch (start us, length us, event | category | flops | bytes accessed | tf_op | source)
XLA Modules:
  0.0 126.9 jit_solution(16665744857769897342)
XLA Ops:
  0.6 120.1 %experts.1 = (bf16[9,256,1024]{2,1,0:T(8,128)(2,1)}, bf16[128,6144]{1,0:T(8,128)(2,1)}, f32[4,6144]{1,0:T(4,128)}, f32[8,128]{1,0:T(8,128)}) custom-call(bf16[128,6144]{1,0:T(8,128)(2,1)} %bitcast.25, s32[2,2,64]{2,1,0:T(2,128)} %bitcast.28, f32[2,2,64]{2,1,0:T(2,128)} %bitcast.29, bf16[9,256,1024]{2,1,0:T(8,128)(2,1)} %bitcast.23, ...), custom_call_target="tpu_custom_call" | custom-call | flops 28991029248 | bytes 200000000 | tf_op jit(solution)/shard_map/experts/pallas_call | solution.py:451
  120.8 5.9 %last.1 = (bf16[9,256,1024]{2,1,0:T(8,128)(2,1)}, bf16[128,6144]{1,0:T(8,128)(2,1)}) custom-call(bf16[9,256,1024]{2,1,0:T(8,128)(2,1)} %get-tuple-element.8.grad_hbm, bf16[128,6144]{1,0:T(8,128)(2,1)} %get-tuple-element.9.tokens_hbm, f32[4,6144]{1,0:T(4,128)} %get-tuple-element.10.router_ref, f32[8,128]{1,0:T(8,128)} %get-tuple-element.11.spread_ref), custom_call_target="tpu_custom_call" | custom-call | tf_op jit(solution)/shard_map/last/pallas_call | solution.py:538

commit v5 on v4

--- a/solution.py
+++ b/solution.py
@@ -20,8 +20,8 @@
 HELD = 6
 PIECES = 4
 FIRST = (
-    "t1", "g12", "x12", "p0", "p2", "x0", "t3", "t5", "p4", "x2", "t7", "p6",
-    "x4", "p8", "x6", "t9", "p10", "x8", "p11", "x10", "x11",
+    "u1", "g12", "x12", "t1", "p0", "p2", "x0", "t3", "t5", "p4", "x2", "t7",
+    "p6", "x4", "p8", "x6", "t9", "p10", "x8", "p11", "x10", "x11",
 )
 EARLY = (
     "r1", "r3", "a0", "r5", "c1", "r7", "c3", "r9", "a2", "c5", "c7", "c9",
@@ -196,7 +196,16 @@
         b = B_CHUNKS.index(k)
         swap_done(k)
         for d in (1, 3):
-            send(x2.at[:, columns(k)], raw_z.at[b, mz], zr.at[k, d - 1], zdev[d], 3)
+            if k == B_CHUNKS[0]:
+                send(x2.at[sib_rows, columns(k)], raw_z.at[b, mz, sib_rows], zr.at[k, d - 1], zdev[d], 3)
+            else:
+                send(x2.at[:, columns(k)], raw_z.at[b, mz], zr.at[k, d - 1], zdev[d], 3)
+
+    def start_own(k):
+        b = B_CHUNKS.index(k)
+        cols = pl.ds(pl.multiple_of(mc * half + k * width, 128), width)
+        for d in (1, 3):
+            send(x_hbm.at[:, cols], raw_z.at[b, mz, mine_rows], zr.at[k, d - 1], zdev[d], 3)
 
     def relay_raw(k):
         b = B_CHUNKS.index(k)
@@ -337,7 +346,7 @@
 
     def in_order(names):
         steps = {
-            "t": start_raw, "r": relay_raw, "c": cross_x, "g": own_select, "p": pack, "x": start_x, "a": around_z,
+            "u": start_own, "t": start_raw, "r": relay_raw, "c": cross_x, "g": own_select, "p": pack, "x": start_x, "a": around_z,
             "n": near, "f": far, "w": whole, "m": compute, "s": near_shared,
         }
         for word in names:

time: 127 us -> 126 us (level)
  no operation moved by 1% of the time
where the time goes in v5:
time: 126 us
  Pallas kernels  125 us (99%)
    pallas_call x1, Pallas kernels, expert_call(): pl.pallas_call(functools.partial(expert_kernel, groups, width), name='exp...  119 us
    pallas_call x1, Pallas kernels, last_call(): pl.pallas_call(last_kernel, name='last', out_shape=(jax.ShapeDtypeStruct(...  5.91 us

profile of v5, /device:TPU:1, one launch (start us, length us, event | category | flops | bytes accessed | tf_op | source)
XLA Modules:
  0.0 125.8 jit_solution(5272314011809833782)
XLA Ops:
  0.6 119.1 %experts.1 = (bf16[9,256,1024]{2,1,0:T(8,128)(2,1)}, bf16[128,6144]{1,0:T(8,128)(2,1)}, f32[4,6144]{1,0:T(4,128)}, f32[8,128]{1,0:T(8,128)}) custom-call(bf16[128,6144]{1,0:T(8,128)(2,1)} %bitcast.25, s32[2,2,64]{2,1,0:T(2,128)} %bitcast.28, f32[2,2,64]{2,1,0:T(2,128)} %bitcast.29, bf16[9,256,1024]{2,1,0:T(8,128)(2,1)} %bitcast.23, ...), custom_call_target="tpu_custom_call" | custom-call | flops 28991029248 | bytes 200000000 | tf_op jit(solution)/shard_map/experts/pallas_call | solution.py:460
  119.7 5.9 %last.1 = (bf16[9,256,1024]{2,1,0:T(8,128)(2,1)}, bf16[128,6144]{1,0:T(8,128)(2,1)}) custom-call(bf16[9,256,1024]{2,1,0:T(8,128)(2,1)} %get-tuple-element.8.grad_hbm, bf16[128,6144]{1,0:T(8,128)(2,1)} %get-tuple-element.9.tokens_hbm, f32[4,6144]{1,0:T(4,128)} %get-tuple-element.10.router_ref, f32[8,128]{1,0:T(8,128)} %get-tuple-element.11.spread_ref), custom_call_target="tpu_custom_call" | custom-call | tf_op jit(solution)/shard_map/last/pallas_call | solution.py:547

commit v6 on v5

--- a/solution.py
+++ b/solution.py
@@ -120,7 +120,7 @@
         own_x[q].start()
 
     barrier = pltpu.get_barrier_semaphore()
-    partners = [sibling, before, after, before_other, after_other] + [dev(mx + dx, mz + dz, mc) for dx, dz in chips]
+    partners = [sibling, before, after, before_other, after_other] + xdev[1:] + zdev[1:]
     for target in partners:
         pl.semaphore_signal(barrier, inc=1, device_id=target, device_id_type=MESH)
     pl.semaphore_wait(barrier, len(partners))

time: 126 us -> 126 us (level)
  no operation moved by 1% of the time
where the time goes in v6:
time: 126 us; the launch traced here: 125 us
  Pallas kernels  125 us (99%)
    pallas_call x1, Pallas kernels, expert_call(): pl.pallas_call(functools.partial(expert_kernel, groups, width), name='exp...  119 us
    pallas_call x1, Pallas kernels, last_call(): pl.pallas_call(last_kernel, name='last', out_shape=(jax.ShapeDtypeStruct(...  5.91 us

profile of v6, /device:TPU:1, one launch (start us, length us, event | category | flops | bytes accessed | tf_op | source)
XLA Modules:
  0.0 125.4 jit_solution(15623157215362212703)
XLA Ops:
  0.6 118.7 %experts.1 = (bf16[9,256,1024]{2,1,0:T(8,128)(2,1)}, bf16[128,6144]{1,0:T(8,128)(2,1)}, f32[4,6144]{1,0:T(4,128)}, f32[8,128]{1,0:T(8,128)}) custom-call(bf16[128,6144]{1,0:T(8,128)(2,1)} %bitcast.25, s32[2,2,64]{2,1,0:T(2,128)} %bitcast.28, f32[2,2,64]{2,1,0:T(2,128)} %bitcast.29, bf16[9,256,1024]{2,1,0:T(8,128)(2,1)} %bitcast.23, ...), custom_call_target="tpu_custom_call" | custom-call | flops 28991029248 | bytes 200000000 | tf_op jit(solution)/shard_map/experts/pallas_call | solution.py:460
  119.3 5.9 %last.1 = (bf16[9,256,1024]{2,1,0:T(8,128)(2,1)}, bf16[128,6144]{1,0:T(8,128)(2,1)}) custom-call(bf16[9,256,1024]{2,1,0:T(8,128)(2,1)} %get-tuple-element.8.grad_hbm, bf16[128,6144]{1,0:T(8,128)(2,1)} %get-tuple-element.9.tokens_hbm, f32[4,6144]{1,0:T(4,128)} %get-tuple-element.10.router_ref, f32[8,128]{1,0:T(8,128)} %get-tuple-element.11.spread_ref), custom_call_target="tpu_custom_call" | custom-call | tf_op jit(solution)/shard_map/last/pallas_call | solution.py:547
